TPU v7x, 256 devices: a whole 4x4x8 slice. The times are simulated.
256 devices in a mesh: tm: 8 (over y, z_lo), chan: 32 (over z_hi, x, core).
Axes of the slice: x: 4, y: 4, z: 8 (z_hi: 4, z_lo: 2; z = z_hi * 2 + z_lo), core: 2. Of those that a mesh axis runs over, the one named last changes fastest.
Arguments:
- recording: float32 [8, 256, 2048], P('tm', 'chan'), may hold values from -22 to 22
- blind_mask: int32 [8, 2048, 256], P('tm', 'chan'), may hold values 0 or 1
- dw_kernels: float32 [3, 32, 9], replicated, may hold values from -2 to 2
- pw_weights: float32 [3, 32, 32], replicated, may hold values from -1 to 1
- biases: float32 [3, 32], replicated, may hold values from -3 to 3
- head_weights: float32 [32], replicated, may hold values from -1 to 1
Outputs:
- dw_grad: float32 [3, 32, 9], replicated
- pw_grad: float32 [3, 32, 32], replicated
- bias_grad: float32 [3, 32], replicated
- head_grad: float32 [32], replicated
- denoised: float32 [8, 256, 2048], P('tm', 'chan')
All inputs are finite; a program needn't handle non-finite values. No bound on the sum of `blind_mask` on one device may be relied on, other than what follows from the above.
Results may differ from a plain program's by a relative error of at most 0.0003.
Values sent between devices are 32-bit elements; how exact they have to be, the bound alone decides.
A program may use at most 128 MiB of HBM per device.

v0:
```python
import functools

import jax
import jax.numpy as jnp
from jax import lax
from jax.experimental import pallas as pl
from jax.experimental.pallas import tpu as pltpu
from jax.sharding import PartitionSpec as P

SPOT_EVERY = 8
F = 32
T = 256
OWN = 64
HALO = 3
OUT = 6
INN = 8
ROWS = OUT * F
COLS = INN * F
NBLK = 11
MESH = pl.DeviceIdType.MESH
F32 = jnp.float32
BF16 = jnp.bfloat16


def iota(shape, dim):
    return lax.broadcasted_iota(jnp.int32, shape, dim)


def split(x):
    hi = x.astype(BF16)
    return hi, (x - hi.astype(F32)).astype(BF16)


def later(x):
    first = iota((x.shape[0], 128), 1) == 0
    a, b = pltpu.roll(x[:, :128], 1, 1), pltpu.roll(x[:, 128:], 1, 1)
    return jnp.concatenate([jnp.where(first, 0.0, a), jnp.where(first, a, b)], axis=1)


def earlier(x):
    last = iota((x.shape[0], 128), 1) == 127
    a, b = pltpu.roll(x[:, :128], 127, 1), pltpu.roll(x[:, 128:], 127, 1)
    return jnp.concatenate([jnp.where(last, b, a), jnp.where(last, 0.0, b)], axis=1)


def dot(a, b):
    return jnp.dot(a, b, preferred_element_type=F32)


def dot_t(a, b):
    return lax.dot_general(a, b, (((1,), (1,)), ((), ())), preferred_element_type=F32)


def as_row(column):
    same = iota((F, COLS), 0) == (iota((F, COLS), 1) & (F - 1))
    return jnp.sum(jnp.where(same, column, 0.0), axis=0, keepdims=True)


def fill_windows(rec_ref, send):
    lane = iota((8, 128), 1)
    tiles = rec_ref.shape[2] // 128
    zero = jnp.zeros((8, 128), F32)
    tile = [rec_ref[0, :, 128 * k : 128 * k + 128] for k in range(tiles)]
    for k in range(tiles):
        before = tile[k - 1] if k > 0 else zero
        after = tile[k + 1] if k < tiles - 1 else zero
        even = jnp.where(lane < HALO, pltpu.roll(before, HALO, 1), pltpu.roll(tile[k], HALO, 1))
        odd = jnp.where(
            lane < OWN + HALO,
            pltpu.roll(tile[k], OWN + HALO, 1),
            pltpu.roll(after, OWN + HALO, 1),
        )
        send[16 * k : 16 * k + 8, :] = even
        send[16 * k + 8 : 16 * k + 16, :] = odd


def comm_in(nchan, rec_ref, mask_ref, win_ref, maskx_ref, send, sems, bsems):
    me = lax.axis_index("chan")
    right, left = lax.rem(me + 1, nchan), lax.rem(me + nchan - 1, nchan)
    barrier = pltpu.get_barrier_semaphore()

    def greet(k, carry):
        pl.semaphore_signal(
            barrier, inc=1, device_id={"chan": lax.rem(me + k, nchan)}, device_id_type=MESH
        )
        return carry

    lax.fori_loop(1, nchan, greet, 0)
    fill_windows(rec_ref, send)
    pl.semaphore_wait(barrier, nchan - 1)

    def tile_copy(peer):
        return pltpu.make_async_remote_copy(
            src_ref=send.at[pl.ds(pl.multiple_of(peer * 8, 8), 8), :],
            dst_ref=win_ref.at[pl.ds(pl.multiple_of(me * 8, 8), 8), :],
            send_sem=sems.at[0],
            recv_sem=sems.at[1],
            device_id={"chan": peer},
            device_id_type=MESH,
        )

    to_right = pltpu.make_async_remote_copy(
        src_ref=mask_ref.at[0, pl.ds(OWN - 8, 8), :],
        dst_ref=maskx_ref.at[pl.ds(0, 8), :],
        send_sem=bsems.at[0],
        recv_sem=bsems.at[1],
        device_id={"chan": right},
        device_id_type=MESH,
    )
    to_left = pltpu.make_async_remote_copy(
        src_ref=mask_ref.at[0, pl.ds(0, 8), :],
        dst_ref=maskx_ref.at[pl.ds(OWN + 8, 8), :],
        send_sem=bsems.at[2],
        recv_sem=bsems.at[3],
        device_id={"chan": left},
        device_id_type=MESH,
    )
    to_right.start()
    to_left.start()

    def push(k, carry):
        tile_copy(lax.rem(me + k, nchan)).start()
        return carry

    lax.fori_loop(1, nchan, push, 0)
    mine = pl.ds(pl.multiple_of(me * 8, 8), 8)
    win_ref[mine, :] = send[mine, :]
    maskx_ref[8 : OWN + 8, :] = mask_ref[0]
    rest = 8 * (nchan - 1)
    every = pltpu.make_async_remote_copy(
        src_ref=send.at[pl.ds(0, rest), :],
        dst_ref=win_ref.at[pl.ds(0, rest), :],
        send_sem=sems.at[0],
        recv_sem=sems.at[1],
        device_id={"chan": right},
        device_id_type=MESH,
    )
    every.wait()
    to_right.wait()
    to_left.wait()


def forward_weights(lhs, pw, dw):
    wide = jnp.concatenate([pw] * INN, axis=1)
    ci = iota((F, COLS), 1) >> 5
    rows = [as_row(dw[:, tap : tap + 1]) for tap in range(9)]
    for j in range(3):
        for co in range(OUT):
            taps = jnp.zeros((F, COLS), F32)
            for i in range(3):
                taps = jnp.where(ci == co + i, rows[3 * i + j], taps)
            hi, lo = split(wide * taps)
            at = slice(j * ROWS + co * F, j * ROWS + co * F + F)
            lhs[at, 0:COLS] = hi
            lhs[at, COLS : 2 * COLS] = lo
            lhs[at, 2 * COLS : 3 * COLS] = hi


def backward_weights(lhs, pw_t, dw):
    wide = jnp.concatenate([pw_t] * INN, axis=1)
    ci = iota((F, COLS), 1) >> 5
    cols = [jnp.broadcast_to(dw[:, tap : tap + 1], (F, COLS)) for tap in range(9)]
    for j in range(3):
        for co in range(OUT):
            taps = jnp.zeros((F, COLS), F32)
            for i in range(3):
                taps = jnp.where(ci == co + 2 - i, cols[3 * i + j], taps)
            hi, lo = split(wide * taps)
            at = slice(j * ROWS + co * F, j * ROWS + co * F + F)
            lhs[at, 0:COLS] = hi
            lhs[at, COLS : 2 * COLS] = lo
            lhs[at, 2 * COLS : 3 * COLS] = hi


def first_weights(lhs, pw, dw):
    lane = iota((F, 144), 1)
    part = (lane >= 48).astype(jnp.int32) + (lane >= 96).astype(jnp.int32)
    spot = lane - 48 * part
    j_of, ci = spot >> 4, spot & 15
    cols = [
        jnp.sum(pw * as_row(dw[:, tap : tap + 1])[:, :F], axis=1, keepdims=True)
        for tap in range(9)
    ]
    for co in range(8):
        taps = jnp.zeros((F, 144), F32)
        for tap in range(9):
            here = (ci == co + tap // 3) & (j_of == tap % 3)
            taps = jnp.where(here, cols[tap], taps)
        hi = taps.astype(BF16).astype(F32)
        lhs[co * F : co * F + F, :] = jnp.where(part == 1, taps - hi, hi).astype(BF16)


def tripled(hi, lo):
    return jnp.concatenate([hi, hi, lo], axis=0)


def silu_parts(pre):
    s = 0.5 * jnp.tanh(0.5 * pre) + 0.5
    a = pre * s
    return a, s + (a - a * s)


def mixed(lhs, hi, lo, flip):
    prod = dot(lhs[...], tripled(hi, lo))
    first, mid, last = prod[:ROWS], prod[ROWS : 2 * ROWS], prod[2 * ROWS :]
    if flip:
        first, last = last, first
    return mid + later(first) + earlier(last)


def fold(x):
    y = x[:, :128] + x[:, 128:]
    y = y + pltpu.roll(y, 64, 1)
    y = y + pltpu.roll(y, 32, 1)
    return y[:, :F]


def shifted_triple(g):
    parts = []
    for x in (earlier(g), g, later(g)):
        hi, lo = split(x)
        parts.append(jnp.concatenate([hi, lo, hi], axis=1))
    return jnp.concatenate(parts, axis=0)


def add_channels(acc, g):
    total = acc[...]
    for k in range(OUT):
        total = total + g[k * F : k * F + F]
    acc[...] = total


def compute(
    nchan, scale, win_ref, maskx_ref, dw_ref, pw_ref, bias_ref, head_ref, out_ref, pack_ref,
    sig, coef, wins, lhs0, lhs_f, lhs_b, a1h, a1l, a2h, a2l, d0, d1,
    g2h, g2l, g1h, g1l, g0h, g0l, acc, acc0, bacc, hacc, bcol, outs,
):
    me = lax.axis_index("chan")
    dw = [dw_ref[l] for l in range(3)]
    pw = [pw_ref[l] for l in range(3)]

    first_weights(lhs0, pw[0], dw[0])
    for l in (1, 2):
        forward_weights(lhs_f.at[l - 1], pw[l], dw[l])
        backward_weights(lhs_b.at[l - 1], pw[l].T, dw[l])
    for l in range(3):
        bcol[l] = jnp.broadcast_to(bias_ref[:, l : l + 1], (F, T))
    bcol[3] = jnp.broadcast_to(head_ref[...], (F, T))

    turned = win_ref[...].T
    sig[...] = turned[:80]
    blind = maskx_ref[5:85, :] == 1
    coef[...] = jnp.where(blind, 2.0 * scale, 0.0)
    act0 = jnp.where(blind, 0.0, turned[:80])
    wins[0] = later(act0)
    wins[1] = act0
    wins[2] = earlier(act0)

    zero2 = jnp.zeros((2 * F, T), BF16)
    for ref in (g2h, g2l, g1h, g1l):
        ref[: 2 * F, :] = zero2
    for ref in (g1h, g1l):
        ref[68 * F :, :] = jnp.zeros((6 * F, T), BF16)
    for ref in (a2h, a2l):
        ref[66 * F :, :] = zero2
    acc[...] = jnp.zeros_like(acc)
    acc0[...] = jnp.zeros_like(acc0)
    bacc[...] = jnp.zeros_like(bacc)
    hacc[...] = jnp.zeros_like(hacc)
    outs[...] = jnp.zeros_like(outs)

    def columns(b):
        return [split(wins[j, pl.ds(pl.multiple_of(8 * b, 8), 16), :]) for j in range(3)]

    def layer0(b, carry):
        parts = columns(b)
        hi = jnp.concatenate([p[0] for p in parts], axis=0)
        lo = jnp.concatenate([p[1] for p in parts], axis=0)
        pre = dot(lhs0[...], tripled(hi, lo))
        pre = pre + jnp.concatenate([bcol[0]] * 8, axis=0)
        a, d = silu_parts(pre)
        at = pl.ds(pl.multiple_of(b * 8 * F, F), 8 * F)
        a1h[at, :], a1l[at, :] = split(a)
        d0[at, :] = d
        return carry

    lax.fori_loop(0, 9, layer0, 0)

    def clear(ends, refs):
        for ref in refs:
            ref[ends, :] = jnp.zeros(((ends.stop - ends.start), T), ref.dtype)

    @pl.when(me == 0)
    def _():
        clear(slice(0, 2 * F), (a1h, a1l, d0))

    @pl.when(me == nchan - 1)
    def _():
        clear(slice(66 * F, 68 * F), (a1h, a1l, d0))

    def inputs(b):
        return pl.ds(pl.multiple_of(b * ROWS, F), COLS)

    def outputs(b, ahead=0):
        return pl.ds(pl.multiple_of(b * ROWS + ahead * F, F), ROWS)

    def layer1(b, carry):
        pre = mixed(lhs_f.at[0], a1h[inputs(b), :], a1l[inputs(b), :], False)
        pre = pre + jnp.concatenate([bcol[1]] * OUT, axis=0)
        a, d = silu_parts(pre)
        a2h[outputs(b), :], a2l[outputs(b), :] = split(a)
        d1[outputs(b), :] = d
        return carry

    lax.fori_loop(0, NBLK, layer1, 0)

    @pl.when(me == 0)
    def _():
        clear(slice(0, F), (a2h, a2l, d1))

    @pl.when(me == nchan - 1)
    def _():
        clear(slice(65 * F, 66 * F), (a2h, a2l, d1))

    par = lax.rem(me, 2) * OWN

    def layer2(b, carry):
        ah, al = a2h[inputs(b), :], a2l[inputs(b), :]
        pre = mixed(lhs_f.at[1], ah, al, False)
        pre = pre + jnp.concatenate([bcol[2]] * OUT, axis=0)
        a, d = silu_parts(pre)
        head = bcol[3]
        heads = hacc[...]
        grads = []
        for k in range(OUT):
            at = slice(k * F, k * F + F)
            row = jnp.sum(head * a[at], axis=0, keepdims=True)
            outs[pl.ds(par + OUT * b + k, 1), :] = row
            spot = pl.ds(OUT * b + k + HALO, 1)
            g_out = jnp.where(OUT * b + k < OWN, coef[spot, :], 0.0) * (row - sig[spot, :])
            heads = heads + g_out * a[at]
            grads.append((head * d[at]) * g_out)
        hacc[...] = heads
        g = jnp.concatenate(grads, axis=0)
        g2h[outputs(b, 2), :], g2l[outputs(b, 2), :] = split(g)
        add_channels(bacc.at[2], g)
        acc[1] += dot_t(shifted_triple(g), jnp.concatenate([ah, ah, al], axis=1))
        return carry

    lax.fori_loop(0, NBLK, layer2, 0)

    out_ref[...] = outs[:128, :].T

    def back2(b, carry):
        g_act = mixed(lhs_b.at[1], g2h[inputs(b), :], g2l[inputs(b), :], True)
        g = g_act * d1[outputs(b), :]
        g1h[outputs(b, 2), :], g1l[outputs(b, 2), :] = split(g)
        add_channels(bacc.at[1], g)
        ah, al = a1h[inputs(b), :], a1l[inputs(b), :]
        acc[0] += dot_t(shifted_triple(g), jnp.concatenate([ah, ah, al], axis=1))
        return carry

    lax.fori_loop(0, NBLK, back2, 0)

    def back1(b, carry):
        g_act = mixed(lhs_b.at[0], g1h[inputs(b), :], g1l[inputs(b), :], True)
        g = g_act * d0[outputs(b), :]
        g0h[outputs(b), :], g0l[outputs(b), :] = split(g)
        add_channels(bacc.at[0], g)
        return carry

    lax.fori_loop(0, NBLK + 1, back1, 0)

    def grads0(b, carry):
        parts = columns(b)
        hi = jnp.concatenate([p[0] for p in parts], axis=0)
        lo = jnp.concatenate([p[1] for p in parts], axis=0)
        at = pl.ds(pl.multiple_of(b * 8 * F, F), 8 * F)
        gh, gl = g0h[at, :], g0l[at, :]
        left = jnp.concatenate([gh, gl, gh], axis=1)
        right = jnp.concatenate([hi, hi, lo], axis=1)
        acc0[...] += dot_t(left, right)
        return carry

    lax.fori_loop(0, 9, grads0, 0)

    ci = iota((F, COLS), 1) >> 5
    pack_rows = []
    pack_pw = []
    lane48 = iota((F, 48), 1)
    taps0 = []
    for tap in range(9):
        total = jnp.zeros((F, 48), F32)
        for co in range(8):
            here = lane48 == (tap % 3) * 16 + co + tap // 3
            total = total + jnp.where(here, acc0[co * F : co * F + F, :], 0.0)
        taps0.append(jnp.sum(total, axis=1, keepdims=True))
    grad_pw = jnp.zeros((F, F), F32)
    for tap in range(9):
        grad_pw = grad_pw + taps0[tap] * as_row(dw[0][:, tap : tap + 1])[:, :F]
        pack_rows.append(jnp.sum(taps0[tap] * pw[0], axis=0, keepdims=True))
    pack_pw.append(grad_pw)
    for l in (1, 2):
        wide = jnp.concatenate([pw[l]] * INN, axis=1)
        grad_pw = jnp.zeros((F, COLS), F32)
        for tap in range(9):
            i, j = tap // 3, tap % 3
            total = jnp.zeros((F, COLS), F32)
            for co in range(OUT):
                at = slice(j * ROWS + co * F, j * ROWS + co * F + F)
                total = total + jnp.where(ci == co + i, acc[l - 1, at, :], 0.0)
            grad_pw = grad_pw + total * as_row(dw[l][:, tap : tap + 1])
            pack_rows.append(fold(jnp.sum(total * wide, axis=0, keepdims=True)))
        pack_pw.append(fold(grad_pw))
    for l in range(3):
        pack_rows.append(as_row(jnp.sum(bacc[l], axis=1, keepdims=True))[:, :F])
    pack_rows.append(as_row(jnp.sum(hacc[...], axis=1, keepdims=True))[:, :F])
    pack_rows.append(jnp.zeros((1, F), F32))
    pack_pw.append(jnp.concatenate(pack_rows, axis=0))
    pack_ref[...] = jnp.concatenate(pack_pw, axis=1)


def comm_out(
    ntm, nchan, outt_ref, pack_ref, dw_out, pw_out, bias_out, head_out, den_out,
    got, r1, r2, r3, v1, v2, dsems, rsems,
):
    me, tm = lax.axis_index("chan"), lax.axis_index("tm")
    near = 8
    far = nchan // near
    barrier = pltpu.get_barrier_semaphore()

    def greet(k, carry):
        pl.semaphore_signal(
            barrier, inc=1, device_id={"chan": lax.rem(me + k, nchan)}, device_id_type=MESH
        )
        return carry

    def greet_tm(k, carry):
        pl.semaphore_signal(
            barrier, inc=1, device_id={"tm": lax.rem(tm + k, ntm)}, device_id_type=MESH
        )
        return carry

    lax.fori_loop(1, ntm, greet_tm, 0)
    lax.fori_loop(1, nchan, greet, 0)
    pl.semaphore_wait(barrier, nchan - 1 + ntm - 1)

    def stage(src, dst, slot, count, where, which):
        def go(k, carry):
            pltpu.make_async_remote_copy(
                src_ref=src,
                dst_ref=dst.at[slot],
                send_sem=rsems.at[which, 0],
                recv_sem=rsems.at[which, 1],
                device_id=where(k),
                device_id_type=MESH,
            ).start()
            return carry

        lax.fori_loop(1, count, go, 0)
        dst[slot] = src[...]

    def finish(dst, count, where, which):
        pltpu.make_async_remote_copy(
            src_ref=dst.at[pl.ds(0, count - 1)],
            dst_ref=dst.at[pl.ds(0, count - 1)],
            send_sem=rsems.at[which, 0],
            recv_sem=rsems.at[which, 1],
            device_id=where(1),
            device_id_type=MESH,
        ).wait()
        total = dst[0]
        for k in range(1, count):
            total = total + dst[k]
        return total

    def by_tm(k):
        return {"tm": lax.rem(tm + k, ntm)}

    base = (me // near) * near

    def by_near(k):
        return {"chan": base + lax.rem(me - base + k, near)}

    def by_far(k):
        return {"chan": lax.rem(me + near * k, nchan)}

    stage(pack_ref, r1, tm, ntm, by_tm, 0)

    def push(k, carry):
        peer = lax.rem(me + k, nchan)
        pltpu.make_async_remote_copy(
            src_ref=outt_ref.at[pl.ds(pl.multiple_of(peer * 8, 8), 8), :],
            dst_ref=got.at[pl.ds(pl.multiple_of(me * 8, 8), 8), :],
            send_sem=dsems.at[0],
            recv_sem=dsems.at[1],
            device_id={"chan": peer},
            device_id_type=MESH,
        ).start()
        return carry

    lax.fori_loop(1, nchan, push, 0)
    mine = pl.ds(pl.multiple_of(me * 8, 8), 8)
    got[mine, :] = outt_ref[mine, :]

    v1[...] = finish(r1, ntm, by_tm, 0)
    stage(v1, r2, me - base, near, by_near, 1)
    v2[...] = finish(r2, near, by_near, 1)
    stage(v2, r3, me // near, far, by_far, 2)

    rest = 8 * (nchan - 1)
    pltpu.make_async_remote_copy(
        src_ref=outt_ref.at[pl.ds(0, rest), :],
        dst_ref=got.at[pl.ds(0, rest), :],
        send_sem=dsems.at[0],
        recv_sem=dsems.at[1],
        device_id={"chan": lax.rem(me + 1, nchan)},
        device_id_type=MESH,
    ).wait()
    lane = iota((8, 128), 1)
    for k in range(nchan // 2):
        den_out[0, :, 128 * k : 128 * k + 128] = jnp.where(
            lane < OWN, got[16 * k : 16 * k + 8, :], got[16 * k + 8 : 16 * k + 16, :]
        )

    total = finish(r3, far, by_far, 2)
    for l in range(3):
        pw_out[l] = total[:, F * l : F * l + F]
    bias_out[...] = total[27:30, 96:128]
    head_out[...] = total[30:31, 96:128]
    padded = jnp.concatenate([total, jnp.zeros((96, 128), F32)], axis=0)
    turned = padded.T
    for l in range(3):
        dw_out[l] = turned[96:128, 9 * l : 9 * l + 9]


def vmem():
    return pl.BlockSpec(memory_space=pltpu.VMEM)


def on_device(ntm, nchan, recording, blind_mask, dw_kernels, pw_weights, biases, head_weights):
    sds = jax.ShapeDtypeStruct
    win, maskx = pl.pallas_call(
        functools.partial(comm_in, nchan),
        out_shape=(sds((T, 128), F32), sds((96, T), jnp.int32)),
        in_specs=[vmem()] * 2,
        out_specs=(vmem(), vmem()),
        scratch_shapes=[
            pltpu.VMEM((T, 128), F32),
            pltpu.SemaphoreType.DMA((2,)),
            pltpu.SemaphoreType.DMA((4,)),
        ],
        compiler_params=pltpu.CompilerParams(collective_id=0, has_side_effects=True),
        name="comm_in",
    )(recording, blind_mask)
    scale = SPOT_EVERY / (ntm * nchan * OWN * T)
    outt, pack = run_compute(
        nchan, scale, win, maskx, dw_kernels, pw_weights, biases, head_weights
    )
    dw_grad, pw_grad, bias_grad, head_grad, denoised = pl.pallas_call(
        functools.partial(comm_out, ntm, nchan),
        out_shape=(
            sds((3, F, 9), F32),
            sds((3, F, F), F32),
            sds((3, F), F32),
            sds((1, F), F32),
            sds((1, 8, OWN * nchan), F32),
        ),
        in_specs=[vmem()] * 2,
        out_specs=(vmem(),) * 5,
        scratch_shapes=[
            pltpu.VMEM((T, 128), F32),
            pltpu.VMEM((ntm, F, 128), F32),
            pltpu.VMEM((8, F, 128), F32),
            pltpu.VMEM((nchan // 8, F, 128), F32),
            pltpu.VMEM((F, 128), F32),
            pltpu.VMEM((F, 128), F32),
            pltpu.SemaphoreType.DMA((2,)),
            pltpu.SemaphoreType.DMA((3, 2)),
        ],
        compiler_params=pltpu.CompilerParams(collective_id=1, has_side_effects=True),
        name="comm_out",
    )(outt, pack)
    return dw_grad, pw_grad, bias_grad, head_grad.reshape(F), denoised


def run_compute(nchan, scale, win, maskx, dw_kernels, pw_weights, biases, head_weights):
    sds = jax.ShapeDtypeStruct
    return pl.pallas_call(
        functools.partial(compute, nchan, scale),
        out_shape=(sds((T, 128), F32), sds((F, 128), F32)),
        in_specs=[vmem()] * 6,
        out_specs=(vmem(), vmem()),
        scratch_shapes=[
            pltpu.VMEM((80, T), F32),
            pltpu.VMEM((80, T), F32),
            pltpu.VMEM((3, 80, T), F32),
            pltpu.VMEM((8 * F, 144), BF16),
            pltpu.VMEM((2, 3 * ROWS, 3 * COLS), BF16),
            pltpu.VMEM((2, 3 * ROWS, 3 * COLS), BF16),
            pltpu.VMEM((72 * F, T), BF16),
            pltpu.VMEM((72 * F, T), BF16),
            pltpu.VMEM((68 * F, T), BF16),
            pltpu.VMEM((68 * F, T), BF16),
            pltpu.VMEM((72 * F, T), F32),
            pltpu.VMEM((66 * F, T), F32),
            pltpu.VMEM((68 * F, T), BF16),
            pltpu.VMEM((68 * F, T), BF16),
            pltpu.VMEM((74 * F, T), BF16),
            pltpu.VMEM((74 * F, T), BF16),
            pltpu.VMEM((72 * F, T), BF16),
            pltpu.VMEM((72 * F, T), BF16),
            pltpu.VMEM((2, 3 * ROWS, COLS), F32),
            pltpu.VMEM((8 * F, 48), F32),
            pltpu.VMEM((3, F, T), F32),
            pltpu.VMEM((F, T), F32),
            pltpu.VMEM((4, F, T), F32),
            pltpu.VMEM((136, T), F32),
        ],
        compiler_params=pltpu.CompilerParams(vmem_limit_bytes=48 << 20),
        name="compute",
    )(win, maskx, dw_kernels, pw_weights, biases.T, head_weights.reshape(F, 1))


def solution(mesh):
    placed = (P("tm", "chan", None), P("tm", "chan", None), P(), P(), P(), P())
    return jax.shard_map(
        functools.partial(on_device, mesh.shape["tm"], mesh.shape["chan"]),
        mesh=mesh,
        in_specs=placed,
        out_specs=(P(), P(), P(), P(), P("tm", "chan", None)),
        check_vma=False,
    )
```

profile of v0, /device:TPU:1, one launch (start us, length us, event | category | flops | bytes accessed | tf_op | source)
XLA Modules:
  0.0 96.2 jit_solution(10479353113532798428)
XLA Ops:
  0.6 0.0 copy-start.7
  0.6 0.8 copy.11
  1.4 0.0 copy-start.9
  1.4 0.7 copy-done.9
  2.1 0.1 copy.13.head_ref
  2.2 0.0 copy-done.7
  2.2 0.1 copy.12.dw_ref
  2.3 0.0 copy-start.3
  2.3 17.0 %comm_in.1 = (f32[256,128]{1,0:T(8,128)}, s32[96,256]{1,0:T(8,128)}) custom-call(f32[1,8,2048]{2,1,0:T(8,128)} %rec_ref.1, s32[1,64,256]{2,1,0:T(8,128)} %mask_ref.1), custom_call_target="tpu_custom_call" | custom-call | tf_op jit(solution)/shard_map/comm_in/pallas_call | solution.py:543
  19.2 0.0 copy-done.3
  19.2 0.0 copy-start.1
  19.2 0.9 copy-done.1
  20.1 0.0 copy-start.2
  20.1 0.9 copy-done.2
  21.0 47.9 %compute.1 = (f32[256,128]{1,0:T(8,128)S(1)}, f32[32,128]{1,0:T(8,128)S(1)}) custom-call(f32[256,128]{1,0:T(8,128)S(1)} %copy-done.1, s32[96,256]{1,0:T(8,128)S(1)} %copy-done.2, f32[3,32,9]{2,1,0:T(8,128)S(1)} %copy.12.dw_ref, f32[3,32,32]{2,1,0:T(8,128)S(1)} %copy-done.3, f32[32,3]{1,0:T(8,128)S(1)} %bitcast.3, f32[32,1]{1,0:T(8,128)S(1)} %copy.13.head_ref), custom_call_target="tpu_custom_call" | custom-call | tf_op jit(solution)/shard_map/compute/pallas_call | solution.py:589
  68.9 0.0 copy-start
  68.9 0.6 copy-done
  69.5 0.6 copy-done.4
  70.2 22.1 %comm_out.1 = (f32[3,32,9]{2,1,0:T(8,128)}, f32[3,32,32]{2,1,0:T(8,128)}, f32[3,32]{1,0:T(4,128)}, f32[1,32]{1,0:T(1,128)}, f32[1,8,2048]{2,1,0:T(8,128)}) custom-call(f32[256,128]{1,0:T(8,128)} %copy-done, f32[32,128]{1,0:T(8,128)} %copy-done.4), custom_call_target="tpu_custom_call" | custom-call | tf_op jit(solution)/shard_map/comm_out/pallas_call | solution.py:560
  92.2 0.0 copy-start.6
  92.2 1.5 %copy.14 = f32[3,32,9]{1,0,2:T(4,128)} copy(f32[3,32,9]{2,1,0:T(8,128)} %get-tuple-element.23) | data formatting | bytes 6912
  93.7 0.0 copy-done.6
  93.7 0.0 copy-start.8
  93.7 0.0 copy-start.5
  93.7 0.6 copy.19
  94.4 0.1 copy-done.8
  94.4 0.0 copy-start.10
  94.4 0.6 copy.20
  95.0 0.0 copy-done.10
  95.0 0.5 copy.21
  95.5 0.0 copy-done.5
  95.5 0.6 copy.22
  (1 shorter events, 0.0 us)
Async XLA Ops:
  0.6 1.5 %copy-start.7 = (f32[3,32,9]{1,0,2:T(4,128)S(1)}, f32[3,32,9]{1,0,2:T(4,128)}, u32[]{:S(2)}) copy-start(f32[3,32,9]{1,0,2:T(4,128)} %param.8) | copy-start | bytes 10372
  1.4 0.7 copy-start.9
  2.3 17.0 %copy-start.3 = (f32[3,32,32]{2,1,0:T(8,128)S(1)}, f32[3,32,32]{2,1,0:T(8,128)}, u32[]{:S(2)}) copy-start(f32[3,32,32]{2,1,0:T(8,128)} %pw_ref.1) | copy-start | bytes 36868
  19.2 0.9 copy-start.1
  20.1 0.9 copy-start.2
  68.9 0.7 copy-start
  69.5 0.6 copy-start.4
  92.2 1.5 %copy-start.6 = (f32[3,32,32]{2,1,0:T(8,128)S(1)}, f32[3,32,32]{2,1,0:T(8,128)}, u32[]{:S(2)}) copy-start(f32[3,32,32]{2,1,0:T(8,128)} %get-tuple-element.34) | copy-start | bytes 36868
  93.7 0.7 copy-start.8
  93.7 1.8 %copy-start.5 = (f32[1,8,2048]{2,1,0:T(8,128)S(1)}, f32[1,8,2048]{2,1,0:T(8,128)}, u32[]{:S(2)}) copy-start(f32[1,8,2048]{2,1,0:T(8,128)} %get-tuple-element.37) | copy-start | bytes 196612
  94.4 0.6 copy-start.10
where the time goes:
time: 96.5 us; the launch traced here: 96.2 us
  Pallas kernels  86.9 us (90%)
  local copies, waits for them, and re-layouts  8.58 us (9%)
    pallas_call x1, Pallas kernels, run_compute(): pl.pallas_call(functools.partial(compute, nchan, scale), out_shape=(sds((...  47.9 us
    pallas_call x1, Pallas kernels, on_device(): pl.pallas_call(functools.partial(comm_out, ntm, nchan), out_shape=(sds((3...  22.1 us
    pallas_call x1, Pallas kernels, on_device(): pl.pallas_call(functools.partial(comm_in, nchan), out_shape=(sds((T, 128)...  17 us
    unnamed x29, local copies, waits for them, and re-layouts  8.5 us

commit v1 on v0

--- a/solution.py
+++ b/solution.py
@@ -20,6 +20,15 @@
 MESH = pl.DeviceIdType.MESH
 F32 = jnp.float32
 BF16 = jnp.bfloat16
+
+
+def aligned(start, size):
+    return start if isinstance(start, int) else pl.multiple_of(start, size)
+
+
+def run(count, body):
+    for b in range(count):
+        body(b)
 
 
 def iota(shape, dim):
@@ -216,10 +225,11 @@
 
 
 def shifted_triple(g):
+    hi, lo = split(g)
     parts = []
-    for x in (earlier(g), g, later(g)):
-        hi, lo = split(x)
-        parts.append(jnp.concatenate([hi, lo, hi], axis=1))
+    for move in (earlier, lambda x: x, later):
+        a, b = move(hi), move(lo)
+        parts.append(jnp.concatenate([a, b, a], axis=1))
     return jnp.concatenate(parts, axis=0)
 
 
@@ -270,21 +280,20 @@
     outs[...] = jnp.zeros_like(outs)
 
     def columns(b):
-        return [split(wins[j, pl.ds(pl.multiple_of(8 * b, 8), 16), :]) for j in range(3)]
-
-    def layer0(b, carry):
+        return [split(wins[j, pl.ds(aligned(8 * b, 8), 16), :]) for j in range(3)]
+
+    def layer0(b):
         parts = columns(b)
         hi = jnp.concatenate([p[0] for p in parts], axis=0)
         lo = jnp.concatenate([p[1] for p in parts], axis=0)
         pre = dot(lhs0[...], tripled(hi, lo))
         pre = pre + jnp.concatenate([bcol[0]] * 8, axis=0)
         a, d = silu_parts(pre)
-        at = pl.ds(pl.multiple_of(b * 8 * F, F), 8 * F)
+        at = pl.ds(aligned(b * 8 * F, F), 8 * F)
         a1h[at, :], a1l[at, :] = split(a)
         d0[at, :] = d
-        return carry
-
-    lax.fori_loop(0, 9, layer0, 0)
+
+    run(9, layer0)
 
     def clear(ends, refs):
         for ref in refs:
@@ -299,20 +308,19 @@
         clear(slice(66 * F, 68 * F), (a1h, a1l, d0))
 
     def inputs(b):
-        return pl.ds(pl.multiple_of(b * ROWS, F), COLS)
+        return pl.ds(aligned(b * ROWS, F), COLS)
 
     def outputs(b, ahead=0):
-        return pl.ds(pl.multiple_of(b * ROWS + ahead * F, F), ROWS)
-
-    def layer1(b, carry):
+        return pl.ds(aligned(b * ROWS + ahead * F, F), ROWS)
+
+    def layer1(b):
         pre = mixed(lhs_f.at[0], a1h[inputs(b), :], a1l[inputs(b), :], False)
         pre = pre + jnp.concatenate([bcol[1]] * OUT, axis=0)
         a, d = silu_parts(pre)
         a2h[outputs(b), :], a2l[outputs(b), :] = split(a)
         d1[outputs(b), :] = d
-        return carry
-
-    lax.fori_loop(0, NBLK, layer1, 0)
+
+    run(NBLK, layer1)
 
     @pl.when(me == 0)
     def _():
@@ -324,7 +332,7 @@
 
     par = lax.rem(me, 2) * OWN
 
-    def layer2(b, carry):
+    def layer2(b):
         ah, al = a2h[inputs(b), :], a2l[inputs(b), :]
         pre = mixed(lhs_f.at[1], ah, al, False)
         pre = pre + jnp.concatenate([bcol[2]] * OUT, axis=0)
@@ -345,44 +353,40 @@
         g2h[outputs(b, 2), :], g2l[outputs(b, 2), :] = split(g)
         add_channels(bacc.at[2], g)
         acc[1] += dot_t(shifted_triple(g), jnp.concatenate([ah, ah, al], axis=1))
-        return carry
-
-    lax.fori_loop(0, NBLK, layer2, 0)
+
+    run(NBLK, layer2)
 
     out_ref[...] = outs[:128, :].T
 
-    def back2(b, carry):
+    def back2(b):
         g_act = mixed(lhs_b.at[1], g2h[inputs(b), :], g2l[inputs(b), :], True)
         g = g_act * d1[outputs(b), :]
         g1h[outputs(b, 2), :], g1l[outputs(b, 2), :] = split(g)
         add_channels(bacc.at[1], g)
         ah, al = a1h[inputs(b), :], a1l[inputs(b), :]
         acc[0] += dot_t(shifted_triple(g), jnp.concatenate([ah, ah, al], axis=1))
-        return carry
-
-    lax.fori_loop(0, NBLK, back2, 0)
-
-    def back1(b, carry):
+
+    run(NBLK, back2)
+
+    def back1(b):
         g_act = mixed(lhs_b.at[0], g1h[inputs(b), :], g1l[inputs(b), :], True)
         g = g_act * d0[outputs(b), :]
         g0h[outputs(b), :], g0l[outputs(b), :] = split(g)
         add_channels(bacc.at[0], g)
-        return carry
-
-    lax.fori_loop(0, NBLK + 1, back1, 0)
-
-    def grads0(b, carry):
+
+    run(NBLK + 1, back1)
+
+    def grads0(b):
         parts = columns(b)
         hi = jnp.concatenate([p[0] for p in parts], axis=0)
         lo = jnp.concatenate([p[1] for p in parts], axis=0)
-        at = pl.ds(pl.multiple_of(b * 8 * F, F), 8 * F)
+        at = pl.ds(aligned(b * 8 * F, F), 8 * F)
         gh, gl = g0h[at, :], g0l[at, :]
         left = jnp.concatenate([gh, gl, gh], axis=1)
         right = jnp.concatenate([hi, hi, lo], axis=1)
         acc0[...] += dot_t(left, right)
-        return carry
-
-    lax.fori_loop(0, 9, grads0, 0)
+
+    run(9, grads0)
 
     ci = iota((F, COLS), 1) >> 5
     pack_rows = []

time: 96.5 us -> 69.9 us (0.72)
  Pallas kernels: 86.9 us -> 60.2 us
    pallas_call x1, Pallas kernels: 47.9 us -> 21.2 us  [run_compute(): pl.pallas_call(functools.partial(compute, nchan, scale), out_shape=(sds((...]
where the time goes in v1:
time: 69.9 us; the launch traced here: 69.5 us
  Pallas kernels  60.2 us (86%)
  local copies, waits for them, and re-layouts  8.6 us (12%)
    pallas_call x1, Pallas kernels, on_device(): pl.pallas_call(functools.partial(comm_out, ntm, nchan), out_shape=(sds((3...  22.1 us
    pallas_call x1, Pallas kernels, run_compute(): pl.pallas_call(functools.partial(compute, nchan, scale), out_shape=(sds((...  21.2 us
    pallas_call x1, Pallas kernels, on_device(): pl.pallas_call(functools.partial(comm_in, nchan), out_shape=(sds((T, 128)...  17 us
    unnamed x29, local copies, waits for them, and re-layouts  8.51 us

profile of v1, /device:TPU:1, one launch (start us, length us, event | category | flops | bytes accessed | tf_op | source)
XLA Modules:
  0.0 69.5 jit_solution(8440676344683963033)
XLA Ops:
  0.6 0.0 copy-start.7
  0.6 0.8 %copy.11 = f32[3,32]{0,1:T(8,128)S(1)} copy(f32[3,32]{1,0:T(4,128)} %param.10) | data formatting | bytes 768 | tf_op args[4]
  1.4 0.0 copy-start.9
  1.4 0.7 copy-done.9
  2.1 0.1 copy.13.head_ref
  2.2 0.0 copy-done.7
  2.2 0.1 copy.12.dw_ref
  2.3 0.0 copy-start.3
  2.3 17.0 %comm_in.1 = (f32[256,128]{1,0:T(8,128)}, s32[96,256]{1,0:T(8,128)}) custom-call(f32[1,8,2048]{2,1,0:T(8,128)} %rec_ref.1, s32[1,64,256]{2,1,0:T(8,128)} %mask_ref.1), custom_call_target="tpu_custom_call" | custom-call | tf_op jit(solution)/shard_map/comm_in/pallas_call | solution.py:547
  19.2 0.0 copy-done.3
  19.2 0.0 copy-start.1
  19.2 0.9 %copy-done.1 = f32[256,128]{1,0:T(8,128)S(1)} copy-done((f32[256,128]{1,0:T(8,128)S(1)}, f32[256,128]{1,0:T(8,128)}, u32[]{:S(2)}) %copy-start.1) | copy-done | bytes 131096
  20.1 0.0 copy-start.2
  20.1 0.9 %copy-done.2 = s32[96,256]{1,0:T(8,128)S(1)} copy-done((s32[96,256]{1,0:T(8,128)S(1)}, s32[96,256]{1,0:T(8,128)}, u32[]{:S(2)}) %copy-start.2) | copy-done | bytes 98328
  21.0 21.2 %compute.1 = (f32[256,128]{1,0:T(8,128)S(1)}, f32[32,128]{1,0:T(8,128)S(1)}) custom-call(f32[256,128]{1,0:T(8,128)S(1)} %copy-done.1, s32[96,256]{1,0:T(8,128)S(1)} %copy-done.2, f32[3,32,9]{2,1,0:T(8,128)S(1)} %copy.12.dw_ref, f32[3,32,32]{2,1,0:T(8,128)S(1)} %copy-done.3, f32[32,3]{1,0:T(8,128)S(1)} %bitcast.3, f32[32,1]{1,0:T(8,128)S(1)} %copy.13.head_ref), custom_call_target="tpu_custom_call" | custom-call | tf_op jit(solution)/shard_map/compute/pallas_call | solution.py:593
  42.2 0.0 copy-start
  42.2 0.7 copy-done
  42.9 0.0 copy-start.4
  42.9 0.6 copy-done.4
  43.5 22.1 %comm_out.1 = (f32[3,32,9]{2,1,0:T(8,128)}, f32[3,32,32]{2,1,0:T(8,128)}, f32[3,32]{1,0:T(4,128)}, f32[1,32]{1,0:T(1,128)}, f32[1,8,2048]{2,1,0:T(8,128)}) custom-call(f32[256,128]{1,0:T(8,128)} %copy-done, f32[32,128]{1,0:T(8,128)} %copy-done.4), custom_call_target="tpu_custom_call" | custom-call | tf_op jit(solution)/shard_map/comm_out/pallas_call | solution.py:564
  65.6 0.0 copy-start.6
  65.6 1.5 %copy.14 = f32[3,32,9]{1,0,2:T(4,128)} copy(f32[3,32,9]{2,1,0:T(8,128)} %get-tuple-element.23) | data formatting | bytes 6912
  67.1 0.0 copy-done.6
  67.1 0.0 copy-start.8
  67.1 0.0 copy-start.5
  67.1 0.6 copy.19
  67.7 0.1 copy-done.8
  67.8 0.6 copy.20
  68.3 0.0 copy-done.10
  68.4 0.5 copy.21
  68.9 0.0 copy-done.5
  68.9 0.6 copy.22
  (1 shorter events, 0.0 us)
Async XLA Ops:
  0.6 1.5 %copy-start.7 = (f32[3,32,9]{1,0,2:T(4,128)S(1)}, f32[3,32,9]{1,0,2:T(4,128)}, u32[]{:S(2)}) copy-start(f32[3,32,9]{1,0,2:T(4,128)} %param.8) | copy-start | bytes 10372
  1.4 0.7 copy-start.9
  2.3 17.0 %copy-start.3 = (f32[3,32,32]{2,1,0:T(8,128)S(1)}, f32[3,32,32]{2,1,0:T(8,128)}, u32[]{:S(2)}) copy-start(f32[3,32,32]{2,1,0:T(8,128)} %pw_ref.1) | copy-start | bytes 36868
  19.2 0.9 %copy-start.1 = (f32[256,128]{1,0:T(8,128)S(1)}, f32[256,128]{1,0:T(8,128)}, u32[]{:S(2)}) copy-start(f32[256,128]{1,0:T(8,128)} %get-tuple-element.14.win_ref) | copy-start | bytes 393220
  20.1 0.9 %copy-start.2 = (s32[96,256]{1,0:T(8,128)S(1)}, s32[96,256]{1,0:T(8,128)}, u32[]{:S(2)}) copy-start(s32[96,256]{1,0:T(8,128)} %get-tuple-element.15.maskx_ref) | copy-start | bytes 294916
  42.2 0.7 copy-start
  42.9 0.6 copy-start.4
  65.6 1.5 %copy-start.6 = (f32[3,32,32]{2,1,0:T(8,128)S(1)}, f32[3,32,32]{2,1,0:T(8,128)}, u32[]{:S(2)}) copy-start(f32[3,32,32]{2,1,0:T(8,128)} %get-tuple-element.34) | copy-start | bytes 36868
  67.1 0.7 copy-start.8
  67.1 1.8 %copy-start.5 = (f32[1,8,2048]{2,1,0:T(8,128)S(1)}, f32[1,8,2048]{2,1,0:T(8,128)}, u32[]{:S(2)}) copy-start(f32[1,8,2048]{2,1,0:T(8,128)} %get-tuple-element.37) | copy-start | bytes 196612
  67.8 0.6 copy-start.10

commit v2 on v1

v2 whole, which is shorter than its diff:
```python
import functools

import jax
import jax.numpy as jnp
from jax import lax
from jax.experimental import pallas as pl
from jax.experimental.pallas import tpu as pltpu
from jax.sharding import PartitionSpec as P

SPOT_EVERY = 8
F = 32
T = 256
OWN = 64
HALO = 3
OUT = 6
INN = 8
ROWS = OUT * F
COLS = INN * F
NBLK = 11
MESH = pl.DeviceIdType.MESH
F32 = jnp.float32
BF16 = jnp.bfloat16


def aligned(start, size):
    return start if isinstance(start, int) else pl.multiple_of(start, size)


def run(count, body):
    for b in range(count):
        body(b)


def iota(shape, dim):
    return lax.broadcasted_iota(jnp.int32, shape, dim)


def split(x):
    hi = x.astype(BF16)
    return hi, (x - hi.astype(F32)).astype(BF16)


def later(x):
    first = iota((x.shape[0], 128), 1) == 0
    a, b = pltpu.roll(x[:, :128], 1, 1), pltpu.roll(x[:, 128:], 1, 1)
    return jnp.concatenate([jnp.where(first, 0.0, a), jnp.where(first, a, b)], axis=1)


def earlier(x):
    last = iota((x.shape[0], 128), 1) == 127
    a, b = pltpu.roll(x[:, :128], 127, 1), pltpu.roll(x[:, 128:], 127, 1)
    return jnp.concatenate([jnp.where(last, b, a), jnp.where(last, 0.0, b)], axis=1)


def dot(a, b):
    return jnp.dot(a, b, preferred_element_type=F32)


def dot_t(a, b):
    return lax.dot_general(a, b, (((1,), (1,)), ((), ())), preferred_element_type=F32)


def repeated(row):
    return jnp.concatenate([row] * INN, axis=1)


def as_column(row):
    return jnp.sum(jnp.where(iota((F, F), 0) == iota((F, F), 1), row, 0.0), axis=1, keepdims=True)


def as_row(column):
    same = iota((F, COLS), 0) == (iota((F, COLS), 1) & (F - 1))
    return jnp.sum(jnp.where(same, column, 0.0), axis=0, keepdims=True)


def fill_windows(rec_ref, send):
    lane = iota((8, 128), 1)
    tiles = rec_ref.shape[2] // 128
    zero = jnp.zeros((8, 128), F32)
    tile = [rec_ref[0, :, 128 * k : 128 * k + 128] for k in range(tiles)]
    for k in range(tiles):
        before = tile[k - 1] if k > 0 else zero
        after = tile[k + 1] if k < tiles - 1 else zero
        even = jnp.where(lane < HALO, pltpu.roll(before, HALO, 1), pltpu.roll(tile[k], HALO, 1))
        odd = jnp.where(
            lane < OWN + HALO,
            pltpu.roll(tile[k], OWN + HALO, 1),
            pltpu.roll(after, OWN + HALO, 1),
        )
        send[16 * k : 16 * k + 8, :] = even
        send[16 * k + 8 : 16 * k + 16, :] = odd


def forward_weights(lhs, pw, dw):
    wide = jnp.concatenate([pw] * INN, axis=1)
    ci = iota((F, COLS), 1) >> 5
    rows = [repeated(row) for row in dw]
    for j in range(3):
        for co in range(OUT):
            taps = jnp.zeros((F, COLS), F32)
            for i in range(3):
                taps = jnp.where(ci == co + i, rows[3 * i + j], taps)
            hi, lo = split(wide * taps)
            at = slice(j * ROWS + co * F, j * ROWS + co * F + F)
            lhs[at, 0:COLS] = hi
            lhs[at, COLS : 2 * COLS] = lo
            lhs[at, 2 * COLS : 3 * COLS] = hi


def backward_weights(lhs, pw_t, dw):
    wide = jnp.concatenate([pw_t] * INN, axis=1)
    ci = iota((F, COLS), 1) >> 5
    cols = [jnp.broadcast_to(as_column(row), (F, COLS)) for row in dw]
    for j in range(3):
        for co in range(OUT):
            taps = jnp.zeros((F, COLS), F32)
            for i in range(3):
                taps = jnp.where(ci == co + 2 - i, cols[3 * i + j], taps)
            hi, lo = split(wide * taps)
            at = slice(j * ROWS + co * F, j * ROWS + co * F + F)
            lhs[at, 0:COLS] = hi
            lhs[at, COLS : 2 * COLS] = lo
            lhs[at, 2 * COLS : 3 * COLS] = hi


def first_weights(lhs, pw, dw):
    lane = iota((F, 144), 1)
    part = (lane >= 48).astype(jnp.int32) + (lane >= 96).astype(jnp.int32)
    spot = lane - 48 * part
    j_of, ci = spot >> 4, spot & 15
    cols = [jnp.sum(pw * row, axis=1, keepdims=True) for row in dw]
    for co in range(8):
        taps = jnp.zeros((F, 144), F32)
        for tap in range(9):
            here = (ci == co + tap // 3) & (j_of == tap % 3)
            taps = jnp.where(here, cols[tap], taps)
        hi = taps.astype(BF16).astype(F32)
        lhs[co * F : co * F + F, :] = jnp.where(part == 1, taps - hi, hi).astype(BF16)


def tripled(hi, lo):
    return jnp.concatenate([hi, hi, lo], axis=0)


def silu_parts(pre):
    s = 0.5 * jnp.tanh(0.5 * pre) + 0.5
    a = pre * s
    return a, s + (a - a * s)


def mixed(lhs, hi, lo, flip):
    prod = dot(lhs[...], tripled(hi, lo))
    first, mid, last = prod[:ROWS], prod[ROWS : 2 * ROWS], prod[2 * ROWS :]
    if flip:
        first, last = last, first
    return mid + later(first) + earlier(last)


def fold(x):
    y = x[:, :128] + x[:, 128:]
    y = y + pltpu.roll(y, 64, 1)
    y = y + pltpu.roll(y, 32, 1)
    return y[:, :F]


def shifted_triple(g):
    hi, lo = split(g)
    parts = []
    for move in (earlier, lambda x: x, later):
        a, b = move(hi), move(lo)
        parts.append(jnp.concatenate([a, b, a], axis=1))
    return jnp.concatenate(parts, axis=0)


def add_channels(acc, g):
    total = acc[...]
    for k in range(OUT):
        total = total + g[k * F : k * F + F]
    acc[...] = total


def step(
    ntm, nchan, scale,
    rec_ref, mask_ref, dw_ref, pw_ref, bias_ref, head_ref,
    dw_out, pw_out, bias_out, head_out, den_out,
    sig, coef, wins, lhs0, lhs_f, lhs_b, a1h, a1l, a2h, a2l, d0, d1,
    g2h, g2l, g1h, g1l, g0h, g0l, acc, acc0, bacc, hacc, bcol, outs,
    send, win, maskx, outt, got, pack, r1, v1, r2, v2, r3, sems,
):
    me, tm = lax.axis_index("chan"), lax.axis_index("tm")
    right, left = lax.rem(me + 1, nchan), lax.rem(me + nchan - 1, nchan)
    barrier = pltpu.get_barrier_semaphore()

    def chan_peer(k):
        return {"chan": lax.rem(me + k, nchan)}

    def tm_peer(k):
        return {"tm": lax.rem(tm + k, ntm)}

    def each(count, go):
        def body(k, carry):
            go(k)
            return carry

        lax.fori_loop(1, count, body, 0)

    def greet(where):
        pl.semaphore_signal(barrier, inc=1, device_id=where, device_id_type=MESH)

    def remote(src, dst, pair, where):
        return pltpu.make_async_remote_copy(
            src_ref=src,
            dst_ref=dst,
            send_sem=sems.at[2 * pair],
            recv_sem=sems.at[2 * pair + 1],
            device_id=where,
            device_id_type=MESH,
        )

    def rows8(index):
        return pl.ds(pl.multiple_of(index * 8, 8), 8)

    def arrived(dst, count, pair, where):
        remote(dst.at[pl.ds(0, count)], dst.at[pl.ds(0, count)], pair, where).wait()

    each(nchan, lambda k: greet(chan_peer(k)))
    each(ntm, lambda k: greet(tm_peer(k)))
    fill_windows(rec_ref, send)
    pl.semaphore_wait(barrier, nchan - 1 + ntm - 1)

    to_right = remote(
        mask_ref.at[0, pl.ds(OWN - 8, 8), :], maskx.at[pl.ds(0, 8), :], 0, {"chan": right}
    )
    to_left = remote(
        mask_ref.at[0, pl.ds(0, 8), :], maskx.at[pl.ds(OWN + 8, 8), :], 1, {"chan": left}
    )

    def push_in(k):
        peer = lax.rem(me + k, nchan)
        remote(send.at[rows8(peer), :], win.at[rows8(me), :], 2, {"chan": peer}).start()

    each(nchan, push_in)
    to_right.start()
    to_left.start()
    win[rows8(me), :] = send[rows8(me), :]
    maskx[8 : OWN + 8, :] = mask_ref[0]
    maskx[OWN + 16 :, :] = jnp.zeros((16, T), jnp.int32)

    dw = [[dw_ref[tap, l : l + 1, :] for tap in range(9)] for l in range(3)]
    pw = [pw_ref[l] for l in range(3)]
    first_weights(lhs0, pw[0], dw[0])
    for l in (1, 2):
        forward_weights(lhs_f.at[l - 1], pw[l], dw[l])
        backward_weights(lhs_b.at[l - 1], pw[l].T, dw[l])
    for l in range(3):
        bcol[l] = jnp.broadcast_to(as_column(bias_ref[l : l + 1, :]), (F, T))
    bcol[3] = jnp.broadcast_to(as_column(head_ref[...]), (F, T))

    zero2 = jnp.zeros((2 * F, T), BF16)
    for ref in (g2h, g2l, g1h, g1l):
        ref[: 2 * F, :] = zero2
    for ref in (g1h, g1l):
        ref[68 * F :, :] = jnp.zeros((6 * F, T), BF16)
    for ref in (a2h, a2l):
        ref[66 * F :, :] = zero2
    acc[...] = jnp.zeros_like(acc)
    acc0[...] = jnp.zeros_like(acc0)
    bacc[...] = jnp.zeros_like(bacc)
    hacc[...] = jnp.zeros_like(hacc)
    outs[...] = jnp.zeros_like(outs)

    to_right.wait()
    to_left.wait()
    arrived(win, 8 * (nchan - 1), 2, {"chan": right})
    turned = win[...].T
    sig[...] = turned[:80]
    blind = maskx[5:85, :] == 1
    coef[...] = jnp.where(blind, 2.0 * scale, 0.0)
    act0 = jnp.where(blind, 0.0, turned[:80])
    wins[0] = later(act0)
    wins[1] = act0
    wins[2] = earlier(act0)

    def columns(b):
        return [split(wins[j, pl.ds(aligned(8 * b, 8), 16), :]) for j in range(3)]

    def layer0(b):
        parts = columns(b)
        hi = jnp.concatenate([p[0] for p in parts], axis=0)
        lo = jnp.concatenate([p[1] for p in parts], axis=0)
        pre = dot(lhs0[...], tripled(hi, lo))
        pre = pre + jnp.concatenate([bcol[0]] * 8, axis=0)
        a, d = silu_parts(pre)
        at = pl.ds(aligned(b * 8 * F, F), 8 * F)
        a1h[at, :], a1l[at, :] = split(a)
        d0[at, :] = d

    run(9, layer0)

    def clear(ends, refs):
        for ref in refs:
            ref[ends, :] = jnp.zeros(((ends.stop - ends.start), T), ref.dtype)

    @pl.when(me == 0)
    def _():
        clear(slice(0, 2 * F), (a1h, a1l, d0))

    @pl.when(me == nchan - 1)
    def _():
        clear(slice(66 * F, 68 * F), (a1h, a1l, d0))

    def inputs(b):
        return pl.ds(aligned(b * ROWS, F), COLS)

    def outputs(b, ahead=0):
        return pl.ds(aligned(b * ROWS + ahead * F, F), ROWS)

    def layer1(b):
        pre = mixed(lhs_f.at[0], a1h[inputs(b), :], a1l[inputs(b), :], False)
        pre = pre + jnp.concatenate([bcol[1]] * OUT, axis=0)
        a, d = silu_parts(pre)
        a2h[outputs(b), :], a2l[outputs(b), :] = split(a)
        d1[outputs(b), :] = d

    run(NBLK, layer1)

    @pl.when(me == 0)
    def _():
        clear(slice(0, F), (a2h, a2l, d1))

    @pl.when(me == nchan - 1)
    def _():
        clear(slice(65 * F, 66 * F), (a2h, a2l, d1))

    par = lax.rem(me, 2) * OWN

    def layer2(b):
        ah, al = a2h[inputs(b), :], a2l[inputs(b), :]
        pre = mixed(lhs_f.at[1], ah, al, False)
        pre = pre + jnp.concatenate([bcol[2]] * OUT, axis=0)
        a, d = silu_parts(pre)
        head = bcol[3]
        heads = hacc[...]
        grads = []
        for k in range(OUT):
            at = slice(k * F, k * F + F)
            row = jnp.sum(head * a[at], axis=0, keepdims=True)
            outs[pl.ds(par + OUT * b + k, 1), :] = row
            spot = pl.ds(OUT * b + k + HALO, 1)
            g_out = jnp.where(OUT * b + k < OWN, coef[spot, :], 0.0) * (row - sig[spot, :])
            heads = heads + g_out * a[at]
            grads.append((head * d[at]) * g_out)
        hacc[...] = heads
        g = jnp.concatenate(grads, axis=0)
        g2h[outputs(b, 2), :], g2l[outputs(b, 2), :] = split(g)
        add_channels(bacc.at[2], g)
        acc[1] += dot_t(shifted_triple(g), jnp.concatenate([ah, ah, al], axis=1))

    run(NBLK, layer2)

    outt[...] = outs[:128, :].T

    def back2(b):
        g_act = mixed(lhs_b.at[1], g2h[inputs(b), :], g2l[inputs(b), :], True)
        g = g_act * d1[outputs(b), :]
        g1h[outputs(b, 2), :], g1l[outputs(b, 2), :] = split(g)
        add_channels(bacc.at[1], g)
        ah, al = a1h[inputs(b), :], a1l[inputs(b), :]
        acc[0] += dot_t(shifted_triple(g), jnp.concatenate([ah, ah, al], axis=1))

    run(NBLK, back2)

    def back1(b):
        g_act = mixed(lhs_b.at[0], g1h[inputs(b), :], g1l[inputs(b), :], True)
        g = g_act * d0[outputs(b), :]
        g0h[outputs(b), :], g0l[outputs(b), :] = split(g)
        add_channels(bacc.at[0], g)

    run(NBLK + 1, back1)

    def grads0(b):
        parts = columns(b)
        hi = jnp.concatenate([p[0] for p in parts], axis=0)
        lo = jnp.concatenate([p[1] for p in parts], axis=0)
        at = pl.ds(aligned(b * 8 * F, F), 8 * F)
        gh, gl = g0h[at, :], g0l[at, :]
        left = jnp.concatenate([gh, gl, gh], axis=1)
        right = jnp.concatenate([hi, hi, lo], axis=1)
        acc0[...] += dot_t(left, right)

    run(9, grads0)

    ci = iota((F, COLS), 1) >> 5
    taps_of = []
    pack_pw = []
    lane48 = iota((F, 48), 1)
    taps0 = []
    for tap in range(9):
        total = jnp.zeros((F, 48), F32)
        for co in range(8):
            here = lane48 == (tap % 3) * 16 + co + tap // 3
            total = total + jnp.where(here, acc0[co * F : co * F + F, :], 0.0)
        taps0.append(jnp.sum(total, axis=1, keepdims=True))
    grad_pw = jnp.zeros((F, F), F32)
    for tap in range(9):
        grad_pw = grad_pw + taps0[tap] * dw[0][tap]
        taps_of.append(jnp.sum(taps0[tap] * pw[0], axis=0, keepdims=True))
    pack_pw.append(grad_pw)
    for l in (1, 2):
        wide = jnp.concatenate([pw[l]] * INN, axis=1)
        grad_pw = jnp.zeros((F, COLS), F32)
        for tap in range(9):
            i, j = tap // 3, tap % 3
            total = jnp.zeros((F, COLS), F32)
            for co in range(OUT):
                at = slice(j * ROWS + co * F, j * ROWS + co * F + F)
                total = total + jnp.where(ci == co + i, acc[l - 1, at, :], 0.0)
            grad_pw = grad_pw + total * repeated(dw[l][tap])
            taps_of.append(fold(jnp.sum(total * wide, axis=0, keepdims=True)))
        pack_pw.append(fold(grad_pw))
    pack_rows = [taps_of[9 * l + tap] for tap in range(9) for l in range(3)]
    for l in range(3):
        pack_rows.append(as_row(jnp.sum(bacc[l], axis=1, keepdims=True))[:, :F])
    pack_rows.append(as_row(jnp.sum(hacc[...], axis=1, keepdims=True))[:, :F])
    pack_rows.append(jnp.zeros((1, F), F32))
    pack_pw.append(jnp.concatenate(pack_rows, axis=0))
    packed = jnp.concatenate(pack_pw, axis=1)
    for k in range(ntm):
        pack[k] = packed[4 * k : 4 * k + 4]

    def scatter(k):
        peer = lax.rem(tm + k, ntm)
        remote(pack.at[peer], r1.at[tm], 3, {"tm": peer}).start()

    each(ntm, scatter)
    r1[tm] = pack[tm]

    def push_out(k):
        peer = lax.rem(me + k, nchan)
        remote(outt.at[rows8(peer), :], got.at[rows8(me), :], 4, {"chan": peer}).start()

    each(nchan, push_out)
    got[rows8(me), :] = outt[rows8(me), :]
    arrived(r1, ntm - 1, 3, tm_peer(1))

    def summed(ref, count):
        total = ref[0]
        for k in range(1, count):
            total = total + ref[k]
        return total

    v1[...] = summed(r1, ntm)
    each(nchan, lambda k: remote(v1, r2.at[me], 5, chan_peer(k)).start())
    r2[me] = v1[...]

    arrived(got, 8 * (nchan - 1), 4, {"chan": right})
    lane = iota((8, 128), 1)
    for k in range(nchan // 2):
        den_out[0, :, 128 * k : 128 * k + 128] = jnp.where(
            lane < OWN, got[16 * k : 16 * k + 8, :], got[16 * k + 8 : 16 * k + 16, :]
        )
    arrived(r2, nchan - 1, 5, {"chan": right})
    v2[...] = summed(r2, nchan)
    each(ntm, lambda k: remote(v2, r3.at[tm], 6, tm_peer(k)).start())
    r3[tm] = v2[...]
    arrived(r3, ntm - 1, 6, tm_peer(1))
    total = jnp.concatenate([r3[k] for k in range(ntm)], axis=0)
    for l in range(3):
        pw_out[l] = total[:, F * l : F * l + F]
    for tap in range(9):
        dw_out[tap] = total[3 * tap : 3 * tap + 3, 3 * F :]
    bias_out[...] = total[27:30, 3 * F :]
    head_out[...] = total[30:31, 3 * F :]


def vmem():
    return pl.BlockSpec(memory_space=pltpu.VMEM)


def on_device(ntm, nchan, recording, blind_mask, dw_kernels, pw_weights, biases, head_weights):
    sds = jax.ShapeDtypeStruct
    scale = SPOT_EVERY / (ntm * nchan * OWN * T)
    dw_grad, pw_grad, bias_grad, head_grad, denoised = pl.pallas_call(
        functools.partial(step, ntm, nchan, scale),
        out_shape=(
            sds((9, 3, F), F32),
            sds((3, F, F), F32),
            sds((3, F), F32),
            sds((1, F), F32),
            sds((1, 8, OWN * nchan), F32),
        ),
        in_specs=[vmem()] * 6,
        out_specs=(vmem(),) * 5,
        scratch_shapes=[
            pltpu.VMEM((80, T), F32),
            pltpu.VMEM((80, T), F32),
            pltpu.VMEM((3, 80, T), F32),
            pltpu.VMEM((8 * F, 144), BF16),
            pltpu.VMEM((2, 3 * ROWS, 3 * COLS), BF16),
            pltpu.VMEM((2, 3 * ROWS, 3 * COLS), BF16),
            pltpu.VMEM((72 * F, T), BF16),
            pltpu.VMEM((72 * F, T), BF16),
            pltpu.VMEM((68 * F, T), BF16),
            pltpu.VMEM((68 * F, T), BF16),
            pltpu.VMEM((72 * F, T), F32),
            pltpu.VMEM((66 * F, T), F32),
            pltpu.VMEM((68 * F, T), BF16),
            pltpu.VMEM((68 * F, T), BF16),
            pltpu.VMEM((74 * F, T), BF16),
            pltpu.VMEM((74 * F, T), BF16),
            pltpu.VMEM((72 * F, T), BF16),
            pltpu.VMEM((72 * F, T), BF16),
            pltpu.VMEM((2, 3 * ROWS, COLS), F32),
            pltpu.VMEM((8 * F, 48), F32),
            pltpu.VMEM((3, F, T), F32),
            pltpu.VMEM((F, T), F32),
            pltpu.VMEM((4, F, T), F32),
            pltpu.VMEM((136, T), F32),
            pltpu.VMEM((T, 128), F32),
            pltpu.VMEM((T, 128), F32),
            pltpu.VMEM((96, T), jnp.int32),
            pltpu.VMEM((T, 128), F32),
            pltpu.VMEM((T, 128), F32),
            pltpu.VMEM((ntm, 4, 128), F32),
            pltpu.VMEM((ntm, 4, 128), F32),
            pltpu.VMEM((4, 128), F32),
            pltpu.VMEM((nchan, 4, 128), F32),
            pltpu.VMEM((4, 128), F32),
            pltpu.VMEM((ntm, 4, 128), F32),
            pltpu.SemaphoreType.DMA((14,)),
        ],
        compiler_params=pltpu.CompilerParams(
            collective_id=0, has_side_effects=True, vmem_limit_bytes=48 << 20
        ),
        name="step",
    )(
        recording,
        blind_mask,
        jnp.transpose(dw_kernels, (2, 0, 1)),
        pw_weights,
        biases,
        head_weights.reshape(1, F),
    )
    return jnp.transpose(dw_grad, (1, 2, 0)), pw_grad, bias_grad, head_grad.reshape(F), denoised


def solution(mesh):
    placed = (P("tm", "chan", None), P("tm", "chan", None), P(), P(), P(), P())
    return jax.shard_map(
        functools.partial(on_device, mesh.shape["tm"], mesh.shape["chan"]),
        mesh=mesh,
        in_specs=placed,
        out_specs=(P(), P(), P(), P(), P("tm", "chan", None)),
        check_vma=False,
    )
```

time: 69.9 us -> 59.7 us (0.85)
  Pallas kernels: 60.2 us -> 51.9 us
  local copies, waits for them, and re-layouts: 8.6 us -> 6.81 us
    pallas_call x3 -> x1, Pallas kernels: 60.2 us -> 51.9 us  [on_device(): pl.pallas_call(functools.partial(step, ntm, nchan, scale), out_shape=(sds...]
    unnamed x29 -> x17, local copies, waits for them, and re-layouts: 8.51 us -> 6.81 us
where the time goes in v2:
time: 59.7 us; the launch traced here: 59.4 us
  Pallas kernels  51.9 us (87%)
  local copies, waits for them, and re-layouts  6.81 us (11%)
  between operations  0.66 us (1%)
    pallas_call x1, Pallas kernels, on_device(): pl.pallas_call(functools.partial(step, ntm, nchan, scale), out_shape=(sds...  51.9 us
    unnamed x17, local copies, waits for them, and re-layouts  6.81 us

profile of v2, /device:TPU:1, one launch (start us, length us, event | category | flops | bytes accessed | tf_op | source)
XLA Modules:
  0.0 59.4 jit_solution(17403432587298400107)
XLA Ops:
  0.6 0.0 copy-start.4
  0.6 0.0 copy-start.5
  0.7 0.7 %copy-done.4 = f32[3,32]{1,0:T(4,128)S(1)} copy-done((f32[3,32]{1,0:T(4,128)S(1)}, f32[3,32]{1,0:T(4,128)}, u32[]{:S(2)}) %copy-start.4) | copy-done | bytes 408
  1.3 0.0 copy-done.5
  1.3 0.0 copy-start
  1.3 0.8 %copy-done = f32[1,8,2048]{2,1,0:T(8,128)S(1)} copy-done((f32[1,8,2048]{2,1,0:T(8,128)S(1)}, f32[1,8,2048]{2,1,0:T(8,128)}, u32[]{:S(2)}) %copy-start) | copy-done | bytes 65560
  2.2 0.0 copy-start.1
  2.2 0.8 %copy-done.1 = s32[1,64,256]{2,1,0:T(8,128)S(1)} copy-done((s32[1,64,256]{2,1,0:T(8,128)S(1)}, s32[1,64,256]{2,1,0:T(8,128)}, u32[]{:S(2)}) %copy-start.1) | copy-done | bytes 65560
  3.0 0.0 copy-start.2
  3.0 0.8 %copy-done.2 = f32[3,32,32]{2,1,0:T(8,128)S(1)} copy-done((f32[3,32,32]{2,1,0:T(8,128)S(1)}, f32[3,32,32]{2,1,0:T(8,128)}, u32[]{:S(2)}) %copy-start.2) | copy-done | bytes 12312
  3.8 0.0 copy-start.3
  3.8 0.7 %copy-done.3 = f32[3,32,9]{1,0,2:T(4,128)S(1)} copy-done((f32[3,32,9]{1,0,2:T(4,128)S(1)}, f32[3,32,9]{1,0,2:T(4,128)}, u32[]{:S(2)}) %copy-start.3) | copy-done | bytes 3480
  4.5 51.9 %step.1 = (f32[9,3,32]{2,1,0:T(4,128)S(1)}, f32[3,32,32]{2,1,0:T(8,128)S(1)}, f32[3,32]{1,0:T(4,128)S(1)}, f32[1,32]{1,0:T(1,128)S(1)}, f32[1,8,2048]{2,1,0:T(8,128)S(1)}) custom-call(f32[1,8,2048]{2,1,0:T(8,128)S(1)} %copy-done, s32[1,64,256]{2,1,0:T(8,128)S(1)} %copy-done.1, f32[9,3,32]{2,1,0:T(4,128)S(1)} %bitcast.4, f32[3,32,32]{2,1,0:T(8,128)S(1)} %copy-done.2, ...), custom_call_target="tpu_custom_call" | custom-call | tf_op jit(solution)/shard_map/step/pallas_call | solution.py:483
  56.4 0.6 %copy.16 = f32[3,32,9]{1,0,2:T(4,128)} copy(f32[3,32,9]{1,0,2:T(4,128)S(1)} %bitcast.5) | data formatting | bytes 6912
  57.0 0.6 %copy.17 = f32[3,32,32]{2,1,0:T(8,128)} copy(f32[3,32,32]{2,1,0:T(8,128)S(1)} %get-tuple-element.21) | data formatting | bytes 24576
  57.6 0.6 copy.18
  58.2 0.5 copy.19
  58.7 0.6 %copy.20 = f32[1,8,2048]{2,1,0:T(8,128)} copy(f32[1,8,2048]{2,1,0:T(8,128)S(1)} %get-tuple-element.24) | data formatting | bytes 131072
Async XLA Ops:
  0.6 0.7 %copy-start.4 = (f32[3,32]{1,0:T(4,128)S(1)}, f32[3,32]{1,0:T(4,128)}, u32[]{:S(2)}) copy-start(f32[3,32]{1,0:T(4,128)} %bias_ref.1) | copy-start | bytes 1156
  0.6 0.7 %copy-start.5 = (f32[32]{0:T(128)S(1)}, f32[32]{0:T(128)}, u32[]{:S(2)}) copy-start(f32[32]{0:T(128)} %param.11) | copy-start | bytes 388
  1.3 0.8 %copy-start = (f32[1,8,2048]{2,1,0:T(8,128)S(1)}, f32[1,8,2048]{2,1,0:T(8,128)}, u32[]{:S(2)}) copy-start(f32[1,8,2048]{2,1,0:T(8,128)} %rec_ref.1) | copy-start | bytes 196612
  2.2 0.8 %copy-start.1 = (s32[1,64,256]{2,1,0:T(8,128)S(1)}, s32[1,64,256]{2,1,0:T(8,128)}, u32[]{:S(2)}) copy-start(s32[1,64,256]{2,1,0:T(8,128)} %mask_ref.1) | copy-start | bytes 196612
  3.0 0.8 %copy-start.2 = (f32[3,32,32]{2,1,0:T(8,128)S(1)}, f32[3,32,32]{2,1,0:T(8,128)}, u32[]{:S(2)}) copy-start(f32[3,32,32]{2,1,0:T(8,128)} %pw_ref.1) | copy-start | bytes 36868
  3.8 0.7 %copy-start.3 = (f32[3,32,9]{1,0,2:T(4,128)S(1)}, f32[3,32,9]{1,0,2:T(4,128)}, u32[]{:S(2)}) copy-start(f32[3,32,9]{1,0,2:T(4,128)} %param.8) | copy-start | bytes 10372

commit v3 on v2

--- a/solution.py
+++ b/solution.py
@@ -181,11 +181,11 @@
 
 def step(
     ntm, nchan, scale,
-    rec_ref, mask_ref, dw_ref, pw_ref, bias_ref, head_ref,
-    dw_out, pw_out, bias_out, head_out, den_out,
+    rec_hbm, mask_hbm, dw_hbm, pw_hbm, bias_hbm, head_hbm, den_out, total_out,
     sig, coef, wins, lhs0, lhs_f, lhs_b, a1h, a1l, a2h, a2l, d0, d1,
     g2h, g2l, g1h, g1l, g0h, g0l, acc, acc0, bacc, hacc, bcol, outs,
-    send, win, maskx, outt, got, pack, r1, v1, r2, v2, r3, sems,
+    rec_ref, dw_ref, pw_ref, bias_ref, head_ref, lsems, send, win, maskx, outt, got,
+    pack, ra, va, rb, vb, rc, pack0, r0a, v0, r0b, sems,
 ):
     me, tm = lax.axis_index("chan"), lax.axis_index("tm")
     right, left = lax.rem(me + 1, nchan), lax.rem(me + nchan - 1, nchan)
@@ -223,16 +223,35 @@
     def arrived(dst, count, pair, where):
         remote(dst.at[pl.ds(0, count)], dst.at[pl.ds(0, count)], pair, where).wait()
 
+    own_rows = pl.ds(8, OWN)
+    loads = [
+        pltpu.make_async_copy(src, dst, lsems.at[k])
+        for k, (src, dst) in enumerate(
+            (
+                (rec_hbm, rec_ref),
+                (mask_hbm.at[0], maskx.at[own_rows, :]),
+                (dw_hbm, dw_ref),
+                (pw_hbm, pw_ref),
+                (bias_hbm, bias_ref),
+                (head_hbm, head_ref),
+            )
+        )
+    ]
+    for load in loads:
+        load.start()
     each(nchan, lambda k: greet(chan_peer(k)))
     each(ntm, lambda k: greet(tm_peer(k)))
+    loads[0].wait()
     fill_windows(rec_ref, send)
+    for load in loads[1:]:
+        load.wait()
     pl.semaphore_wait(barrier, nchan - 1 + ntm - 1)
 
     to_right = remote(
-        mask_ref.at[0, pl.ds(OWN - 8, 8), :], maskx.at[pl.ds(0, 8), :], 0, {"chan": right}
+        maskx.at[pl.ds(OWN, 8), :], maskx.at[pl.ds(0, 8), :], 0, {"chan": right}
     )
     to_left = remote(
-        mask_ref.at[0, pl.ds(0, 8), :], maskx.at[pl.ds(OWN + 8, 8), :], 1, {"chan": left}
+        maskx.at[pl.ds(8, 8), :], maskx.at[pl.ds(OWN + 8, 8), :], 1, {"chan": left}
     )
 
     def push_in(k):
@@ -243,7 +262,6 @@
     to_right.start()
     to_left.start()
     win[rows8(me), :] = send[rows8(me), :]
-    maskx[8 : OWN + 8, :] = mask_ref[0]
     maskx[OWN + 16 :, :] = jnp.zeros((16, T), jnp.int32)
 
     dw = [[dw_ref[tap, l : l + 1, :] for tap in range(9)] for l in range(3)]
@@ -368,44 +386,14 @@
         ah, al = a1h[inputs(b), :], a1l[inputs(b), :]
         acc[0] += dot_t(shifted_triple(g), jnp.concatenate([ah, ah, al], axis=1))
 
+    def push_out(k):
+        peer = lax.rem(me + k, nchan)
+        remote(outt.at[rows8(peer), :], got.at[rows8(me), :], 4, {"chan": peer}).start()
+
     run(NBLK, back2)
 
-    def back1(b):
-        g_act = mixed(lhs_b.at[0], g1h[inputs(b), :], g1l[inputs(b), :], True)
-        g = g_act * d0[outputs(b), :]
-        g0h[outputs(b), :], g0l[outputs(b), :] = split(g)
-        add_channels(bacc.at[0], g)
-
-    run(NBLK + 1, back1)
-
-    def grads0(b):
-        parts = columns(b)
-        hi = jnp.concatenate([p[0] for p in parts], axis=0)
-        lo = jnp.concatenate([p[1] for p in parts], axis=0)
-        at = pl.ds(aligned(b * 8 * F, F), 8 * F)
-        gh, gl = g0h[at, :], g0l[at, :]
-        left = jnp.concatenate([gh, gl, gh], axis=1)
-        right = jnp.concatenate([hi, hi, lo], axis=1)
-        acc0[...] += dot_t(left, right)
-
-    run(9, grads0)
-
     ci = iota((F, COLS), 1) >> 5
-    taps_of = []
-    pack_pw = []
-    lane48 = iota((F, 48), 1)
-    taps0 = []
-    for tap in range(9):
-        total = jnp.zeros((F, 48), F32)
-        for co in range(8):
-            here = lane48 == (tap % 3) * 16 + co + tap // 3
-            total = total + jnp.where(here, acc0[co * F : co * F + F, :], 0.0)
-        taps0.append(jnp.sum(total, axis=1, keepdims=True))
-    grad_pw = jnp.zeros((F, F), F32)
-    for tap in range(9):
-        grad_pw = grad_pw + taps0[tap] * dw[0][tap]
-        taps_of.append(jnp.sum(taps0[tap] * pw[0], axis=0, keepdims=True))
-    pack_pw.append(grad_pw)
+    rows_of, pack_pw = {}, []
     for l in (1, 2):
         wide = jnp.concatenate([pw[l]] * INN, axis=1)
         grad_pw = jnp.zeros((F, COLS), F32)
@@ -416,32 +404,15 @@
                 at = slice(j * ROWS + co * F, j * ROWS + co * F + F)
                 total = total + jnp.where(ci == co + i, acc[l - 1, at, :], 0.0)
             grad_pw = grad_pw + total * repeated(dw[l][tap])
-            taps_of.append(fold(jnp.sum(total * wide, axis=0, keepdims=True)))
+            rows_of[l, tap] = fold(jnp.sum(total * wide, axis=0, keepdims=True))
         pack_pw.append(fold(grad_pw))
-    pack_rows = [taps_of[9 * l + tap] for tap in range(9) for l in range(3)]
-    for l in range(3):
-        pack_rows.append(as_row(jnp.sum(bacc[l], axis=1, keepdims=True))[:, :F])
-    pack_rows.append(as_row(jnp.sum(hacc[...], axis=1, keepdims=True))[:, :F])
-    pack_rows.append(jnp.zeros((1, F), F32))
+    pack_rows = [rows_of[l, tap] for tap in range(9) for l in (1, 2)]
+    for sums in (bacc[1], bacc[2], hacc[...]):
+        pack_rows.append(as_row(jnp.sum(sums, axis=1, keepdims=True))[:, :F])
+    pack_rows.append(jnp.zeros((F - 21, F), F32))
     pack_pw.append(jnp.concatenate(pack_rows, axis=0))
-    packed = jnp.concatenate(pack_pw, axis=1)
-    for k in range(ntm):
-        pack[k] = packed[4 * k : 4 * k + 4]
-
-    def scatter(k):
-        peer = lax.rem(tm + k, ntm)
-        remote(pack.at[peer], r1.at[tm], 3, {"tm": peer}).start()
-
-    each(ntm, scatter)
-    r1[tm] = pack[tm]
-
-    def push_out(k):
-        peer = lax.rem(me + k, nchan)
-        remote(outt.at[rows8(peer), :], got.at[rows8(me), :], 4, {"chan": peer}).start()
-
-    each(nchan, push_out)
-    got[rows8(me), :] = outt[rows8(me), :]
-    arrived(r1, ntm - 1, 3, tm_peer(1))
+    pack_pw.append(jnp.zeros((F, F), F32))
+    pack[...] = jnp.concatenate(pack_pw, axis=1)
 
     def summed(ref, count):
         total = ref[0]
@@ -449,28 +420,110 @@
             total = total + ref[k]
         return total
 
-    v1[...] = summed(r1, ntm)
-    each(nchan, lambda k: remote(v1, r2.at[me], 5, chan_peer(k)).start())
-    r2[me] = v1[...]
+    near = 8
+    far = nchan // near
+    base = (me // near) * near
+
+    def near_peer(k):
+        return {"chan": base + lax.rem(me - base + k, near)}
+
+    def far_peer(k):
+        return {"chan": lax.rem(me + near * k, nchan)}
+
+    def back1(b):
+        g_act = mixed(lhs_b.at[0], g1h[inputs(b), :], g1l[inputs(b), :], True)
+        g = g_act * d0[outputs(b), :]
+        g0h[outputs(b), :], g0l[outputs(b), :] = split(g)
+        add_channels(bacc.at[0], g)
+
+    each(ntm, lambda k: remote(pack, ra.at[tm], 3, tm_peer(k)).start())
+    ra[tm] = pack[...]
+    run(NBLK + 1, back1)
+
+    def grads0(b):
+        parts = columns(b)
+        hi = jnp.concatenate([p[0] for p in parts], axis=0)
+        lo = jnp.concatenate([p[1] for p in parts], axis=0)
+        at = pl.ds(aligned(b * 8 * F, F), 8 * F)
+        gh, gl = g0h[at, :], g0l[at, :]
+        left = jnp.concatenate([gh, gl, gh], axis=1)
+        right = jnp.concatenate([hi, hi, lo], axis=1)
+        acc0[...] += dot_t(left, right)
+
+    run(9, grads0)
+
+    lane48 = iota((F, 48), 1)
+    firsts = []
+    for tap in range(9):
+        total = jnp.zeros((F, 48), F32)
+        for co in range(8):
+            here = lane48 == (tap % 3) * 16 + co + tap // 3
+            total = total + jnp.where(here, acc0[co * F : co * F + F, :], 0.0)
+        firsts.append(as_row(jnp.sum(total, axis=1, keepdims=True))[:, :128])
+    firsts.append(as_row(jnp.sum(bacc[0], axis=1, keepdims=True))[:, :128])
+    group = iota((1, 128), 1) >> 5
+    for r in range(3):
+        row = jnp.zeros((1, 128), F32)
+        for q, first in enumerate(firsts[4 * r : 4 * r + 4]):
+            row = jnp.where(group == q, first, row)
+        pack0[r : r + 1, :] = row
+    pack0[3:4, :] = jnp.zeros((1, 128), F32)
+    each(ntm, lambda k: remote(pack0, r0a.at[tm], 7, tm_peer(k)).start())
+    r0a[tm] = pack0[...]
+
+    each(nchan, push_out)
+    got[rows8(me), :] = outt[rows8(me), :]
+    arrived(ra, ntm - 1, 3, tm_peer(1))
+    va[...] = summed(ra, ntm)
+    each(near, lambda k: remote(va, rb.at[me - base], 5, near_peer(k)).start())
+    rb[me - base] = va[...]
+
+    arrived(r0a, ntm - 1, 7, tm_peer(1))
+    v0[...] = summed(r0a, ntm)
+    each(nchan, lambda k: remote(v0, r0b.at[me], 8, chan_peer(k)).start())
+    r0b[me] = v0[...]
+
+    arrived(rb, near - 1, 5, near_peer(1))
+    vb[...] = summed(rb, near)
+    each(far, lambda k: remote(vb, rc.at[me // near], 6, far_peer(k)).start())
+    rc[me // near] = vb[...]
 
     arrived(got, 8 * (nchan - 1), 4, {"chan": right})
     lane = iota((8, 128), 1)
     for k in range(nchan // 2):
-        den_out[0, :, 128 * k : 128 * k + 128] = jnp.where(
+        den_out[:, 128 * k : 128 * k + 128] = jnp.where(
             lane < OWN, got[16 * k : 16 * k + 8, :], got[16 * k + 8 : 16 * k + 16, :]
         )
-    arrived(r2, nchan - 1, 5, {"chan": right})
-    v2[...] = summed(r2, nchan)
-    each(ntm, lambda k: remote(v2, r3.at[tm], 6, tm_peer(k)).start())
-    r3[tm] = v2[...]
-    arrived(r3, ntm - 1, 6, tm_peer(1))
-    total = jnp.concatenate([r3[k] for k in range(ntm)], axis=0)
-    for l in range(3):
-        pw_out[l] = total[:, F * l : F * l + F]
+    arrived(r0b, nchan - 1, 8, {"chan": right})
+    sums = summed(r0b, nchan)
+    rows = [sums[k // 4 : k // 4 + 1, F * (k % 4) : F * (k % 4) + F] for k in range(10)]
+    grad_pw = jnp.zeros((F, F), F32)
+    final_rows = []
     for tap in range(9):
-        dw_out[tap] = total[3 * tap : 3 * tap + 3, 3 * F :]
-    bias_out[...] = total[27:30, 3 * F :]
-    head_out[...] = total[30:31, 3 * F :]
+        column = as_column(rows[tap])
+        grad_pw = grad_pw + column * dw[0][tap]
+        final_rows.append(jnp.sum(column * pw[0], axis=0, keepdims=True))
+    final_rows.append(rows[9])
+    final_rows.append(jnp.zeros((1, F), F32))
+    arrived(rc, far - 1, 6, far_peer(1))
+    later_layers = summed(rc, far)
+    all_rows = jnp.concatenate([later_layers[:21, 2 * F : 3 * F]] + final_rows, axis=0)
+    total_out[...] = jnp.concatenate([later_layers[:, : 2 * F], all_rows, grad_pw], axis=1)
+
+
+def unpack(den_ref, total_ref, dw_out, pw_out, bias_out, head_out, den_out):
+    den_out[0] = den_ref[...]
+    total = total_ref[...]
+    pw_out[0] = total[:, 3 * F :]
+    pw_out[1] = total[:, :F]
+    pw_out[2] = total[:, F : 2 * F]
+    rows = total[:, 2 * F : 3 * F]
+    for tap in range(9):
+        dw_out[tap, 0:1, :] = rows[21 + tap : 22 + tap]
+        dw_out[tap, 1:3, :] = rows[2 * tap : 2 * tap + 2]
+    bias_out[0:1, :] = rows[30:31]
+    bias_out[1:3, :] = rows[18:20]
+    head_out[...] = rows[20:21]
 
 
 def vmem():
@@ -480,17 +533,11 @@
 def on_device(ntm, nchan, recording, blind_mask, dw_kernels, pw_weights, biases, head_weights):
     sds = jax.ShapeDtypeStruct
     scale = SPOT_EVERY / (ntm * nchan * OWN * T)
-    dw_grad, pw_grad, bias_grad, head_grad, denoised = pl.pallas_call(
+    den, total = pl.pallas_call(
         functools.partial(step, ntm, nchan, scale),
-        out_shape=(
-            sds((9, 3, F), F32),
-            sds((3, F, F), F32),
-            sds((3, F), F32),
-            sds((1, F), F32),
-            sds((1, 8, OWN * nchan), F32),
-        ),
-        in_specs=[vmem()] * 6,
-        out_specs=(vmem(),) * 5,
+        out_shape=(sds((8, OWN * nchan), F32), sds((F, 128), F32)),
+        in_specs=[pl.BlockSpec(memory_space=pltpu.HBM)] * 6,
+        out_specs=(vmem(),) * 2,
         scratch_shapes=[
             pltpu.VMEM((80, T), F32),
             pltpu.VMEM((80, T), F32),
@@ -516,21 +563,31 @@
             pltpu.VMEM((F, T), F32),
             pltpu.VMEM((4, F, T), F32),
             pltpu.VMEM((136, T), F32),
+            pltpu.VMEM((1, 8, OWN * nchan), F32),
+            pltpu.VMEM((9, 3, F), F32),
+            pltpu.VMEM((3, F, F), F32),
+            pltpu.VMEM((3, F), F32),
+            pltpu.VMEM((1, F), F32),
+            pltpu.SemaphoreType.DMA((6,)),
             pltpu.VMEM((T, 128), F32),
             pltpu.VMEM((T, 128), F32),
             pltpu.VMEM((96, T), jnp.int32),
             pltpu.VMEM((T, 128), F32),
             pltpu.VMEM((T, 128), F32),
-            pltpu.VMEM((ntm, 4, 128), F32),
+            pltpu.VMEM((F, 128), F32),
+            pltpu.VMEM((ntm, F, 128), F32),
+            pltpu.VMEM((F, 128), F32),
+            pltpu.VMEM((8, F, 128), F32),
+            pltpu.VMEM((F, 128), F32),
+            pltpu.VMEM((nchan // 8, F, 128), F32),
+            pltpu.VMEM((4, 128), F32),
             pltpu.VMEM((ntm, 4, 128), F32),
             pltpu.VMEM((4, 128), F32),
             pltpu.VMEM((nchan, 4, 128), F32),
-            pltpu.VMEM((4, 128), F32),
-            pltpu.VMEM((ntm, 4, 128), F32),
-            pltpu.SemaphoreType.DMA((14,)),
+            pltpu.SemaphoreType.DMA((18,)),
         ],
         compiler_params=pltpu.CompilerParams(
-            collective_id=0, has_side_effects=True, vmem_limit_bytes=48 << 20
+            collective_id=0, has_side_effects=True, vmem_limit_bytes=62 << 20
         ),
         name="step",
     )(
@@ -541,6 +598,20 @@
         biases,
         head_weights.reshape(1, F),
     )
+    dw_grad, pw_grad, bias_grad, head_grad, denoised = pl.pallas_call(
+        unpack,
+        out_shape=(
+            sds((9, 3, F), F32),
+            sds((3, F, F), F32),
+            sds((3, F), F32),
+            sds((1, F), F32),
+            sds((1, 8, OWN * nchan), F32),
+        ),
+        in_specs=[vmem()] * 2,
+        out_specs=(vmem(),) * 5,
+        compiler_params=pltpu.CompilerParams(vmem_limit_bytes=62 << 20),
+        name="unpack",
+    )(den, total)
     return jnp.transpose(dw_grad, (1, 2, 0)), pw_grad, bias_grad, head_grad.reshape(F), denoised
 
 

time: 59.7 us -> 53.8 us (0.901)
  local copies, waits for them, and re-layouts: 6.81 us -> 0 us
  Pallas kernels: 51.9 us -> 53 us
    unnamed x17 -> x0, local copies, waits for them, and re-layouts: 6.81 us -> none
    pallas_call x0 -> x1, Pallas kernels: none -> 1.57 us  [on_device(): pl.pallas_call(unpack, out_shape=(sds((9, 3, F), F32), sds((3, F, F), F32...]
where the time goes in v3:
time: 53.8 us; the launch traced here: 53.7 us
  Pallas kernels  53 us (99%)
  between operations  0.64 us (1%)
    pallas_call x1, Pallas kernels, on_device(): pl.pallas_call(functools.partial(step, ntm, nchan, scale), out_shape=(sds...  51.4 us
    pallas_call x1, Pallas kernels, on_device(): pl.pallas_call(unpack, out_shape=(sds((9, 3, F), F32), sds((3, F, F), F32...  1.57 us

profile of v3, /device:TPU:1, one launch (start us, length us, event | category | flops | bytes accessed | tf_op | source)
XLA Modules:
  0.0 53.7 jit_solution(11549576657484140620)
XLA Ops:
  0.6 51.4 %step.1 = (f32[8,2048]{1,0:T(8,128)}, f32[32,128]{1,0:T(8,128)}) custom-call(f32[1,8,2048]{2,1,0:T(8,128)} %rec_hbm.1, s32[1,64,256]{2,1,0:T(8,128)} %mask_hbm.1, f32[9,3,32]{2,1,0:T(4,128)} %bitcast.4, f32[3,32,32]{2,1,0:T(8,128)} %pw_hbm.1, f32[3,32]{1,0:T(4,128)} %bias_hbm.1, f32[1,32]{1,0:T(1,128)} %bitcast.5), custom_call_target="tpu_custom_call" | custom-call | tf_op jit(solution)/shard_map/step/pallas_call | solution.py:536
  52.1 1.6 %unpack.1 = (f32[9,3,32]{2,1,0:T(4,128)}, f32[3,32,32]{2,1,0:T(8,128)}, f32[3,32]{1,0:T(4,128)}, f32[1,32]{1,0:T(1,128)}, f32[1,8,2048]{2,1,0:T(8,128)}) custom-call(f32[8,2048]{1,0:T(8,128)} %get-tuple-element.12.den_ref, f32[32,128]{1,0:T(8,128)} %get-tuple-element.13.total_ref), custom_call_target="tpu_custom_call" | custom-call | tf_op jit(solution)/shard_map/unpack/pallas_call | solution.py:601

commit v4 on v3

--- a/solution.py
+++ b/solution.py
@@ -29,6 +29,14 @@
 def run(count, body):
     for b in range(count):
         body(b)
+
+
+def without(x, start, stop, outside):
+    parts = [x[: start * F]] if start else []
+    parts.append(jnp.where(outside, 0.0, x[start * F : stop * F]))
+    if stop * F < x.shape[0]:
+        parts.append(x[stop * F :])
+    return jnp.concatenate(parts, axis=0)
 
 
 def iota(shape, dim):
@@ -204,6 +212,16 @@
 
         lax.fori_loop(1, count, body, 0)
 
+    def each_chan(go):
+        others = nchan - 8
+
+        def body(k, carry):
+            go(8 + lax.rem(k + 8, others))
+            return carry
+
+        lax.fori_loop(0, others, body, 0)
+        each(8, go)
+
     def greet(where):
         pl.semaphore_signal(barrier, inc=1, device_id=where, device_id_type=MESH)
 
@@ -239,7 +257,7 @@
     ]
     for load in loads:
         load.start()
-    each(nchan, lambda k: greet(chan_peer(k)))
+    each_chan(lambda k: greet(chan_peer(k)))
     each(ntm, lambda k: greet(tm_peer(k)))
     loads[0].wait()
     fill_windows(rec_ref, send)
@@ -258,7 +276,7 @@
         peer = lax.rem(me + k, nchan)
         remote(send.at[rows8(peer), :], win.at[rows8(me), :], 2, {"chan": peer}).start()
 
-    each(nchan, push_in)
+    each_chan(push_in)
     to_right.start()
     to_left.start()
     win[rows8(me), :] = send[rows8(me), :]
@@ -309,23 +327,15 @@
         pre = dot(lhs0[...], tripled(hi, lo))
         pre = pre + jnp.concatenate([bcol[0]] * 8, axis=0)
         a, d = silu_parts(pre)
+        if b == 0:
+            a, d = (without(x, 0, 2, me == 0) for x in (a, d))
+        if b == 8:
+            a, d = (without(x, 2, 4, me == nchan - 1) for x in (a, d))
         at = pl.ds(aligned(b * 8 * F, F), 8 * F)
         a1h[at, :], a1l[at, :] = split(a)
         d0[at, :] = d
 
     run(9, layer0)
-
-    def clear(ends, refs):
-        for ref in refs:
-            ref[ends, :] = jnp.zeros(((ends.stop - ends.start), T), ref.dtype)
-
-    @pl.when(me == 0)
-    def _():
-        clear(slice(0, 2 * F), (a1h, a1l, d0))
-
-    @pl.when(me == nchan - 1)
-    def _():
-        clear(slice(66 * F, 68 * F), (a1h, a1l, d0))
 
     def inputs(b):
         return pl.ds(aligned(b * ROWS, F), COLS)
@@ -337,18 +347,14 @@
         pre = mixed(lhs_f.at[0], a1h[inputs(b), :], a1l[inputs(b), :], False)
         pre = pre + jnp.concatenate([bcol[1]] * OUT, axis=0)
         a, d = silu_parts(pre)
+        if b == 0:
+            a, d = (without(x, 0, 1, me == 0) for x in (a, d))
+        if b == NBLK - 1:
+            a, d = (without(x, 5, 6, me == nchan - 1) for x in (a, d))
         a2h[outputs(b), :], a2l[outputs(b), :] = split(a)
         d1[outputs(b), :] = d
 
     run(NBLK, layer1)
-
-    @pl.when(me == 0)
-    def _():
-        clear(slice(0, F), (a2h, a2l, d1))
-
-    @pl.when(me == nchan - 1)
-    def _():
-        clear(slice(65 * F, 66 * F), (a2h, a2l, d1))
 
     par = lax.rem(me, 2) * OWN
 
@@ -471,16 +477,16 @@
     each(ntm, lambda k: remote(pack0, r0a.at[tm], 7, tm_peer(k)).start())
     r0a[tm] = pack0[...]
 
-    each(nchan, push_out)
-    got[rows8(me), :] = outt[rows8(me), :]
     arrived(ra, ntm - 1, 3, tm_peer(1))
     va[...] = summed(ra, ntm)
     each(near, lambda k: remote(va, rb.at[me - base], 5, near_peer(k)).start())
     rb[me - base] = va[...]
 
+    each(nchan, push_out)
+    got[rows8(me), :] = outt[rows8(me), :]
     arrived(r0a, ntm - 1, 7, tm_peer(1))
     v0[...] = summed(r0a, ntm)
-    each(nchan, lambda k: remote(v0, r0b.at[me], 8, chan_peer(k)).start())
+    each_chan(lambda k: remote(v0, r0b.at[me], 8, chan_peer(k)).start())
     r0b[me] = v0[...]
 
     arrived(rb, near - 1, 5, near_peer(1))

time: 53.8 us -> 52.2 us (0.970)
  Pallas kernels: 53 us -> 51.3 us
    pallas_call x1, Pallas kernels: 51.4 us -> 49.8 us  [on_device(): pl.pallas_call(functools.partial(step, ntm, nchan, scale), out_shape=(sds...]
where the time goes in v4:
time: 52.2 us; the launch traced here: 52 us
  Pallas kernels  51.3 us (98%)
  between operations  0.64 us (1%)
    pallas_call x1, Pallas kernels, on_device(): pl.pallas_call(functools.partial(step, ntm, nchan, scale), out_shape=(sds...  49.8 us
    pallas_call x1, Pallas kernels, on_device(): pl.pallas_call(unpack, out_shape=(sds((9, 3, F), F32), sds((3, F, F), F32...  1.57 us

profile of v4, /device:TPU:1, one launch (start us, length us, event | category | flops | bytes accessed | tf_op | source)
XLA Modules:
  0.0 52.0 jit_solution(5927318778036285130)
XLA Ops:
  0.6 49.8 %step.1 = (f32[8,2048]{1,0:T(8,128)}, f32[32,128]{1,0:T(8,128)}) custom-call(f32[1,8,2048]{2,1,0:T(8,128)} %rec_hbm.1, s32[1,64,256]{2,1,0:T(8,128)} %mask_hbm.1, f32[9,3,32]{2,1,0:T(4,128)} %bitcast.4, f32[3,32,32]{2,1,0:T(8,128)} %pw_hbm.1, f32[3,32]{1,0:T(4,128)} %bias_hbm.1, f32[1,32]{1,0:T(1,128)} %bitcast.5), custom_call_target="tpu_custom_call" | custom-call | tf_op jit(solution)/shard_map/step/pallas_call | solution.py:542
  50.4 1.6 %unpack.1 = (f32[9,3,32]{2,1,0:T(4,128)}, f32[3,32,32]{2,1,0:T(8,128)}, f32[3,32]{1,0:T(4,128)}, f32[1,32]{1,0:T(1,128)}, f32[1,8,2048]{2,1,0:T(8,128)}) custom-call(f32[8,2048]{1,0:T(8,128)} %get-tuple-element.12.den_ref, f32[32,128]{1,0:T(8,128)} %get-tuple-element.13.total_ref), custom_call_target="tpu_custom_call" | custom-call | tf_op jit(solution)/shard_map/unpack/pallas_call | solution.py:607

commit v5 on v4

--- a/solution.py
+++ b/solution.py
@@ -299,7 +299,6 @@
         ref[68 * F :, :] = jnp.zeros((6 * F, T), BF16)
     for ref in (a2h, a2l):
         ref[66 * F :, :] = zero2
-    acc[...] = jnp.zeros_like(acc)
     acc0[...] = jnp.zeros_like(acc0)
     bacc[...] = jnp.zeros_like(bacc)
     hacc[...] = jnp.zeros_like(hacc)
@@ -378,7 +377,8 @@
         g = jnp.concatenate(grads, axis=0)
         g2h[outputs(b, 2), :], g2l[outputs(b, 2), :] = split(g)
         add_channels(bacc.at[2], g)
-        acc[1] += dot_t(shifted_triple(g), jnp.concatenate([ah, ah, al], axis=1))
+        part = dot_t(shifted_triple(g), jnp.concatenate([ah, ah, al], axis=1))
+        acc[1] = part if b == 0 else acc[1] + part
 
     run(NBLK, layer2)
 
@@ -390,7 +390,8 @@
         g1h[outputs(b, 2), :], g1l[outputs(b, 2), :] = split(g)
         add_channels(bacc.at[1], g)
         ah, al = a1h[inputs(b), :], a1l[inputs(b), :]
-        acc[0] += dot_t(shifted_triple(g), jnp.concatenate([ah, ah, al], axis=1))
+        part = dot_t(shifted_triple(g), jnp.concatenate([ah, ah, al], axis=1))
+        acc[0] = part if b == 0 else acc[0] + part
 
     def push_out(k):
         peer = lax.rem(me + k, nchan)
@@ -473,7 +474,6 @@
         for q, first in enumerate(firsts[4 * r : 4 * r + 4]):
             row = jnp.where(group == q, first, row)
         pack0[r : r + 1, :] = row
-    pack0[3:4, :] = jnp.zeros((1, 128), F32)
     each(ntm, lambda k: remote(pack0, r0a.at[tm], 7, tm_peer(k)).start())
     r0a[tm] = pack0[...]
 
@@ -586,10 +586,10 @@
             pltpu.VMEM((8, F, 128), F32),
             pltpu.VMEM((F, 128), F32),
             pltpu.VMEM((nchan // 8, F, 128), F32),
-            pltpu.VMEM((4, 128), F32),
-            pltpu.VMEM((ntm, 4, 128), F32),
-            pltpu.VMEM((4, 128), F32),
-            pltpu.VMEM((nchan, 4, 128), F32),
+            pltpu.VMEM((3, 128), F32),
+            pltpu.VMEM((ntm, 3, 128), F32),
+            pltpu.VMEM((3, 128), F32),
+            pltpu.VMEM((nchan, 3, 128), F32),
             pltpu.SemaphoreType.DMA((18,)),
         ],
         compiler_params=pltpu.CompilerParams(

time: 52.2 us -> 52 us (level)
  no operation moved by 1% of the time
where the time goes in v5:
time: 52 us; the launch traced here: 51.8 us
  Pallas kernels  51.2 us (98%)
  between operations  0.64 us (1%)
    pallas_call x1, Pallas kernels, on_device(): pl.pallas_call(functools.partial(step, ntm, nchan, scale), out_shape=(sds...  49.6 us
    pallas_call x1, Pallas kernels, on_device(): pl.pallas_call(unpack, out_shape=(sds((9, 3, F), F32), sds((3, F, F), F32...  1.57 us

profile of v5, /device:TPU:1, one launch (start us, length us, event | category | flops | bytes accessed | tf_op | source)
XLA Modules:
  0.0 51.8 jit_solution(14782346588818593780)
XLA Ops:
  0.6 49.6 %step.1 = (f32[8,2048]{1,0:T(8,128)}, f32[32,128]{1,0:T(8,128)}) custom-call(f32[1,8,2048]{2,1,0:T(8,128)} %rec_hbm.1, s32[1,64,256]{2,1,0:T(8,128)} %mask_hbm.1, f32[9,3,32]{2,1,0:T(4,128)} %bitcast.4, f32[3,32,32]{2,1,0:T(8,128)} %pw_hbm.1, f32[3,32]{1,0:T(4,128)} %bias_hbm.1, f32[1,32]{1,0:T(1,128)} %bitcast.5), custom_call_target="tpu_custom_call" | custom-call | tf_op jit(solution)/shard_map/step/pallas_call | solution.py:542
  50.3 1.6 %unpack.1 = (f32[9,3,32]{2,1,0:T(4,128)}, f32[3,32,32]{2,1,0:T(8,128)}, f32[3,32]{1,0:T(4,128)}, f32[1,32]{1,0:T(1,128)}, f32[1,8,2048]{2,1,0:T(8,128)}) custom-call(f32[8,2048]{1,0:T(8,128)} %get-tuple-element.12.den_ref, f32[32,128]{1,0:T(8,128)} %get-tuple-element.13.total_ref), custom_call_target="tpu_custom_call" | custom-call | tf_op jit(solution)/shard_map/unpack/pallas_call | solution.py:607
